TPU v7x, 32 devices: a whole 2x2x4 slice. The times are simulated.
32 devices in a mesh: ctx: 8 (over z, x), head: 4 (over y, core).
Axes of the slice: x: 2, y: 2, z: 4, core: 2. Of those that a mesh axis runs over, the one named last changes fastest.
Arguments:
- query: bfloat16 [4096, 1024], P('ctx', 'head'), may hold values from -7.5 to 7.5
- key: bfloat16 [4096, 1024], P('ctx', 'head'), may hold values from -7.5 to 7.5
- value: bfloat16 [4096, 1024], P('ctx', 'head'), may hold values from -6 to 6
- grad_out: bfloat16 [4096, 1024], P('ctx', 'head'), may hold values from -6 to 6
- picks: int32 [32, 16, 4], P('ctx', 'head'), may hold values from 0 to 7, as said below
Outputs:
- attn_out: bfloat16 [4096, 1024], P('ctx', 'head')
- grad_query: bfloat16 [4096, 1024], P('ctx', 'head')
- grad_key: bfloat16 [4096, 1024], P('ctx', 'head')
- grad_value: bfloat16 [4096, 1024], P('ctx', 'head')
Inputs may be any that keep to these rules, and one draw needn't show every extreme that they name: picks[g, h, 0] is the block that holds tile g; every other entry is that block again (no further block) or an earlier block. Among the tiles of one block and one group of 4 consecutive heads, no earlier block is named twice.
All inputs are finite; a program needn't handle non-finite values.
Results may differ from a plain program's by a relative error of at most 0.017.
Values may be sent and summed in bfloat16 or wider, within the bound.
No kernel may reach another device: no remote copies, remote signals or barrier semaphores. Data moves between devices by JAX's collectives and lax.ppermute only.
A program may use at most 64 MiB of HBM per device.

v0:
```python
import math

import jax
import jax.numpy as jnp
from jax import lax
from jax.sharding import PartitionSpec as P

masked_value = -1e30
highest = lax.Precision.HIGHEST


def attend_slots(q_slots, head_ids, k_heads, v_heads, scaling):
    key_rows = jnp.take(k_heads, head_ids, axis=0)
    value_rows = jnp.take(v_heads, head_ids, axis=0)
    scores = (
        jnp.einsum("ndq,nkd->nqk", q_slots, key_rows, preferred_element_type=jnp.float32) * scaling
    )
    peak_score = jnp.max(scores, axis=-1, keepdims=True)
    log_total = peak_score + jnp.log(jnp.sum(jnp.exp(scores - peak_score), axis=-1, keepdims=True))
    attend_low = jnp.exp(scores - log_total).astype(jnp.bfloat16)
    outputs = jnp.einsum("nqk,nkd->ndq", attend_low, value_rows, preferred_element_type=jnp.float32)
    return (outputs, log_total[..., 0])


def slot_grads(q_slots, g_slots, c_slots, lse_slots, head_ids, k_heads, v_heads, scaling):
    key_rows = jnp.take(k_heads, head_ids, axis=0)
    value_rows = jnp.take(v_heads, head_ids, axis=0)
    scores = (
        jnp.einsum("ndq,nkd->nqk", q_slots, key_rows, preferred_element_type=jnp.float32) * scaling
    )
    attend = jnp.exp(scores - lse_slots[..., None])
    attend_low = attend.astype(jnp.bfloat16)
    grad_v = jnp.einsum("nqk,ndq->nkd", attend_low, g_slots, preferred_element_type=jnp.float32)
    grad_prob = jnp.einsum("ndq,nkd->nqk", g_slots, value_rows, preferred_element_type=jnp.float32)
    dscore = (attend * (grad_prob - c_slots[..., None])).astype(jnp.bfloat16)
    grad_k = (
        jnp.einsum("nqk,ndq->nkd", dscore, q_slots, preferred_element_type=jnp.float32) * scaling
    )
    grad_q = (
        jnp.einsum("nqk,nkd->ndq", dscore, key_rows, preferred_element_type=jnp.float32) * scaling
    )
    return (grad_k, grad_v, grad_q)


def local(query, key, value, grad_out, picks):
    row_count, columns = query.shape
    tiles_dev, groups, picked = picks.shape
    head_dim = columns // groups
    tile_rows = row_count // tiles_dev
    others = picked - 1
    scaling = 1.0 / math.sqrt(head_dim)
    devices = lax.axis_size("ctx")
    own_block = lax.axis_index("ctx")
    per_group = min(8, devices)
    all_picks = lax.all_gather(picks, "ctx", axis=0, tiled=True)
    q_heads = query.reshape(row_count, groups, head_dim).transpose(1, 0, 2)
    k_heads = key.reshape(row_count, groups, head_dim).transpose(1, 0, 2)
    v_heads = value.reshape(row_count, groups, head_dim).transpose(1, 0, 2)
    q_tiles = query.reshape(tiles_dev, tile_rows, groups, head_dim)
    do_tiles = grad_out.reshape(tiles_dev, tile_rows, groups, head_dim)
    do_major = do_tiles.transpose(0, 2, 1, 3)
    positions = jnp.arange(row_count, dtype=jnp.int32)
    tile_masks = []
    for tile_step in range(tiles_dev):
        span = (tile_step + 1) * tile_rows
        query_pos = positions[tile_step * tile_rows : span]
        tile_masks.append(positions[None, :span] <= query_pos[:, None])
    targets = picks[:, :, 1:]
    active = targets != own_block
    lookup = jnp.where(active, targets, own_block).reshape(-1)
    peer_ids = jnp.arange(devices, dtype=jnp.int32)
    routing = ((targets[None] == peer_ids[:, None, None, None]) & active[None]).astype(jnp.float32)
    routing_low = routing.astype(jnp.bfloat16)
    send_q = jnp.einsum(
        "jtgi,tqgd->jdq", routing_low, q_tiles, preferred_element_type=jnp.float32
    ).astype(jnp.bfloat16)
    recv_q = lax.all_to_all(send_q, "ctx", split_axis=0, concat_axis=0, tiled=True)

    def own_forward(inputs):
        q_head, k_head, v_head = inputs
        out_list = []
        lse_list = []
        for tile_step in range(tiles_dev):
            span = (tile_step + 1) * tile_rows
            q_part = q_head[tile_step * tile_rows : span]
            scores = (
                jnp.einsum("qd,kd->qk", q_part, k_head[:span], preferred_element_type=jnp.float32)
                * scaling
            )
            scores = jnp.where(tile_masks[tile_step], scores, masked_value)
            peak_score = jnp.max(scores, axis=-1, keepdims=True)
            log_total = peak_score + jnp.log(
                jnp.sum(jnp.exp(scores - peak_score), axis=-1, keepdims=True)
            )
            attend_low = jnp.exp(scores - log_total).astype(jnp.bfloat16)
            out_list.append(jnp.dot(attend_low, v_head[:span], preferred_element_type=jnp.float32))
            lse_list.append(log_total[:, 0])
        return (jnp.concatenate(out_list, axis=0), jnp.concatenate(lse_list, axis=0))

    own_out, own_lse = lax.map(own_forward, (q_heads, k_heads, v_heads))
    sources = all_picks.reshape(devices, tiles_dev, groups, picked)[..., 1:]
    incoming = (sources == own_block) & (peer_ids[:, None, None, None] != own_block)
    live_in = jnp.any(incoming, axis=(1, 2, 3))
    group_ids = jnp.arange(groups, dtype=jnp.int32)
    head_of = jnp.sum(jnp.where(incoming, group_ids[None, None, :, None], 0), axis=(1, 2, 3))
    ranking = jnp.argsort(jnp.where(live_in, 0, 1) * devices + peer_ids)
    inverse = jnp.argsort(ranking)
    rounds = (jnp.sum(live_in.astype(jnp.int32)) + per_group - 1) // per_group
    heads_sorted = jnp.take(head_of, ranking, axis=0)
    q_sorted = jnp.take(recv_q, ranking, axis=0)

    def forward_turn(turn, totals):
        served_out, served_lse = totals
        offset = turn * per_group
        query_part = lax.dynamic_slice_in_dim(q_sorted, offset, per_group, 0)
        head_part = lax.dynamic_slice_in_dim(heads_sorted, offset, per_group, 0)
        out_part, lse_part = attend_slots(query_part, head_part, k_heads, v_heads, scaling)
        served_out = lax.dynamic_update_slice_in_dim(served_out, out_part, offset, 0)
        served_lse = lax.dynamic_update_slice_in_dim(served_lse, lse_part, offset, 0)
        return (served_out, served_lse)

    start_fwd = (
        jnp.zeros((devices, head_dim, tile_rows), jnp.float32),
        jnp.zeros((devices, tile_rows), jnp.float32),
    )
    served_out, served_lse = lax.fori_loop(0, rounds, forward_turn, start_fwd)
    back_out, back_lse = (
        lax.all_to_all(
            jnp.take(served_out, inverse, axis=0), "ctx", split_axis=0, concat_axis=0, tiled=True
        ),
        lax.all_to_all(
            jnp.take(served_lse, inverse, axis=0), "ctx", split_axis=0, concat_axis=0, tiled=True
        ),
    )
    task_out = jnp.take(back_out, lookup, axis=0).reshape(
        tiles_dev, groups, others, head_dim, tile_rows
    )
    task_lse = jnp.take(back_lse, lookup, axis=0).reshape(tiles_dev, groups, others, tile_rows)
    own_out_t = own_out.reshape(groups, tiles_dev, tile_rows, head_dim).transpose(1, 0, 2, 3)
    own_lse_t = own_lse.reshape(groups, tiles_dev, tile_rows).transpose(1, 0, 2)
    active_rows = active[..., None]
    rem_lse = jnp.where(active_rows, task_lse, masked_value)
    ceiling = jnp.maximum(own_lse_t, jnp.max(rem_lse, axis=2))
    log_total = ceiling + jnp.log(
        jnp.exp(own_lse_t - ceiling) + jnp.sum(jnp.exp(rem_lse - ceiling[:, :, None]), axis=2)
    )
    own_weight = jnp.exp(own_lse_t - log_total)
    rem_weight = jnp.where(active_rows, jnp.exp(rem_lse - log_total[:, :, None]), 0.0)
    mixed = own_weight[..., None] * own_out_t + jnp.einsum(
        "tgiq,tgidq->tgqd", rem_weight, task_out, precision=highest
    )
    out_low = mixed.astype(jnp.bfloat16)
    attn_out = out_low.transpose(0, 2, 1, 3).reshape(row_count, columns)
    row_delta = jnp.sum(do_major.astype(jnp.float32) * out_low.astype(jnp.float32), axis=-1)
    own_scaled = (own_weight[..., None] * do_major.astype(jnp.float32)).astype(jnp.bfloat16)
    own_shift = own_weight * row_delta
    g_heads = own_scaled.transpose(1, 0, 2, 3).reshape(groups, row_count, head_dim)
    c_heads = own_shift.transpose(1, 0, 2).reshape(groups, row_count)

    def own_backward(inputs):
        q_head, k_head, v_head, g_head, c_head, lse_head = inputs
        grad_k = jnp.zeros((row_count, head_dim), jnp.float32)
        grad_v = jnp.zeros((row_count, head_dim), jnp.float32)
        dq_list = []
        for tile_step in range(tiles_dev):
            first = tile_step * tile_rows
            span = (tile_step + 1) * tile_rows
            q_part = q_head[first:span]
            g_part = g_head[first:span]
            k_part = k_head[:span]
            scores = (
                jnp.einsum("qd,kd->qk", q_part, k_part, preferred_element_type=jnp.float32)
                * scaling
            )
            scores = jnp.where(tile_masks[tile_step], scores, masked_value)
            attend = jnp.exp(scores - lse_head[first:span, None])
            attend_low = attend.astype(jnp.bfloat16)
            part_dv = jnp.einsum(
                "qk,qd->kd", attend_low, g_part, preferred_element_type=jnp.float32
            )
            grad_prob = jnp.einsum(
                "qd,kd->qk", g_part, v_head[:span], preferred_element_type=jnp.float32
            )
            dscore = (attend * (grad_prob - c_head[first:span, None])).astype(jnp.bfloat16)
            part_dk = (
                jnp.einsum("qk,qd->kd", dscore, q_part, preferred_element_type=jnp.float32)
                * scaling
            )
            dq_list.append(jnp.dot(dscore, k_part, preferred_element_type=jnp.float32) * scaling)
            padding = ((0, row_count - span), (0, 0))
            grad_k = grad_k + jnp.pad(part_dk, padding)
            grad_v = grad_v + jnp.pad(part_dv, padding)
        return (grad_k, grad_v, jnp.concatenate(dq_list, axis=0))

    own_dk, own_dv, own_dq = lax.map(
        own_backward, (q_heads, k_heads, v_heads, g_heads, c_heads, own_lse)
    )
    rem_shift = rem_weight * row_delta[:, :, None]
    rem_scaled = (rem_weight[..., None] * do_major[:, :, None].astype(jnp.float32)).astype(
        jnp.bfloat16
    )
    send_g = jnp.einsum(
        "jtgi,tgiqd->jdq", routing_low, rem_scaled, preferred_element_type=jnp.float32
    )
    send_c = jnp.einsum("jtgi,tgiq->jq", routing, rem_shift, precision=highest)
    recv_g, recv_c = (
        lax.all_to_all(send_g, "ctx", split_axis=0, concat_axis=0, tiled=True),
        lax.all_to_all(send_c, "ctx", split_axis=0, concat_axis=0, tiled=True),
    )
    g_sorted = jnp.take(recv_g, ranking, axis=0).astype(jnp.bfloat16)
    c_sorted = jnp.take(recv_c, ranking, axis=0)

    def backward_turn(turn, totals):
        grad_k, grad_v, served_dq = totals
        offset = turn * per_group
        query_part = lax.dynamic_slice_in_dim(q_sorted, offset, per_group, 0)
        cot_part = lax.dynamic_slice_in_dim(g_sorted, offset, per_group, 0)
        shift_part = lax.dynamic_slice_in_dim(c_sorted, offset, per_group, 0)
        lse_part = lax.dynamic_slice_in_dim(served_lse, offset, per_group, 0)
        head_part = lax.dynamic_slice_in_dim(heads_sorted, offset, per_group, 0)
        part_dk, part_dv, part_dq = slot_grads(
            query_part, cot_part, shift_part, lse_part, head_part, k_heads, v_heads, scaling
        )
        head_onehot = (head_part[:, None] == group_ids[None, :]).astype(jnp.float32)
        grad_k = grad_k + jnp.einsum("ng,nkd->gkd", head_onehot, part_dk, precision=highest)
        grad_v = grad_v + jnp.einsum("ng,nkd->gkd", head_onehot, part_dv, precision=highest)
        served_dq = lax.dynamic_update_slice_in_dim(served_dq, part_dq, offset, 0)
        return (grad_k, grad_v, served_dq)

    zeros_heads = jnp.zeros((groups, row_count, head_dim), jnp.float32)
    start_bwd = (zeros_heads, zeros_heads, jnp.zeros((devices, head_dim, tile_rows), jnp.float32))
    rem_dk, rem_dv, served_dq = lax.fori_loop(0, rounds, backward_turn, start_bwd)
    back_dq = lax.all_to_all(
        jnp.take(served_dq, inverse, axis=0).astype(jnp.bfloat16),
        "ctx",
        split_axis=0,
        concat_axis=0,
        tiled=True,
    ).astype(jnp.float32)
    task_dq = jnp.take(back_dq, lookup, axis=0).reshape(
        tiles_dev, groups, others, head_dim, tile_rows
    )
    rem_dq = jnp.sum(jnp.where(active[..., None, None], task_dq, 0.0), axis=2)
    own_dq_t = own_dq.reshape(groups, tiles_dev, tile_rows, head_dim).transpose(1, 0, 2, 3)
    total_dq = own_dq_t + rem_dq.transpose(0, 1, 3, 2)
    grad_query = total_dq.transpose(0, 2, 1, 3).reshape(row_count, columns).astype(jnp.bfloat16)
    grad_key = (own_dk + rem_dk).transpose(1, 0, 2).reshape(row_count, columns).astype(jnp.bfloat16)
    grad_value = (
        (own_dv + rem_dv).transpose(1, 0, 2).reshape(row_count, columns).astype(jnp.bfloat16)
    )
    return (attn_out, grad_query, grad_key, grad_value)


def solution(mesh):
    placed = (
        P("ctx", "head"),
        P("ctx", "head"),
        P("ctx", "head"),
        P("ctx", "head"),
        P("ctx", "head", None),
    )
    return jax.shard_map(
        local,
        mesh=mesh,
        in_specs=placed,
        out_specs=(P("ctx", "head"), P("ctx", "head"), P("ctx", "head"), P("ctx", "head")),
        check_vma=False,
    )
```

profile of v0, /device:TPU:0, one launch (start us, length us, event | category | flops | bytes accessed | tf_op | source)
XLA Modules:
  0.0 241.5 jit_solution(6803299519002546479)
XLA Ops:
  5.9 7.3 %all-to-all-start = ((bf16[8,64,128]{2,1,0:T(8,128)(2,1)}), bf16[8,64,128]{2,1,0:T(8,128)(2,1)S(1)}, u32[]{:S(2)}, u32[]{:S(2)}) async-start(bf16[8,64,128]{2,1,0:T(8,128)(2,1)} %copy.160), calls=%async_computation | async-start | bytes 262144 | tf_op jit(solution)/shard_map/all_to_all | solution.py:77
  13.2 31.1 %all_gather.3 = s32[32,4,4]{2,1,0:T(4,128)S(1)} all-gather(s32[4,4,4]{2,1,0:T(4,128)S(1)} %copy-done.30), channel_id=1, replica_groups=mesh['ctx'=8,'head'=4] {'ctx'}, dimensions={0}, use_global_device_ids=true | all-gather | bytes 2304 | tf_op jit(solution)/shard_map/all_gather | solution.py:55
  52.8 10.9 %while.67 = (s32[]{:T(128)}, f32[4,512,64]{1,2,0:T(8,128)S(1)}, f32[4,512]{1,0:T(4,128)S(1)}, bf16[4,512,64]{2,1,0:T(8,128)(2,1)S(1)}, bf16[4,512,64]{2,1,0:T(8,...) while((s32[]{:T(128)}, f32[4,512,64]{1,2,0:T(8,128)S(1)}, ...), condition=%wide.region_9.10_spmd.clone, body=%wide.region_0.9_spmd.clone.sunk | while | flops 43353092 | bytes 3178213 | solution.py:100
  78.0 4.2 %all-to-all-start.1 = ((f32[8,1,128]{2,1,0:T(1,128)}), f32[8,1,128]{2,1,0:T(1,128)S(1)}, u32[]{:S(2)}, u32[]{:S(2)}) async-start(f32[8,1,128]{2,1,0:T(1,128)} %bitcast.19), calls=%async_computation.1 | async-start | bytes 8192 | tf_op jit(solution)/shard_map/all_to_all | solution.py:131
  82.2 1.6 gather_fusion.6
  84.7 4.0 %all-to-all-done.1 = f32[8,1,128]{2,1,0:T(1,128)S(1)} async-done(((f32[8,1,128]{2,1,0:T(1,128)}), f32[8,1,128]{2,1,0:T(1,128)S(1)}, u32[]{:S(2)}, u32[]{:S(2)}) %all-to-all-start.1) | async-done | bytes 4128 | tf_op jit(solution)/shard_map/all_to_all | solution.py:131
  91.1 3.4 %all-to-all-start.3 = ((bf16[8,64,128]{2,1,0:T(8,128)(2,1)}), bf16[8,64,128]{2,1,0:T(8,128)(2,1)S(1)}, u32[]{:S(2)}, u32[]{:S(2)}) async-start(bf16[8,64,128]{2,1,0:T(8,128)(2,1)} %copy.173), calls=%async_computation.3 | async-start | bytes 262144 | tf_op jit(solution)/shard_map/all_to_all | solution.py:207
  96.4 6.1 %all-to-all-done.3 = bf16[8,64,128]{2,1,0:T(8,128)(2,1)S(1)} async-done(((bf16[8,64,128]{2,1,0:T(8,128)(2,1)}), bf16[8,64,128]{2,1,0:T(8,128)(2,1)S(1)}, u32[]{:S(2)}, u32[]{:S(2)}) %all-to-all-start.3) | async-done | bytes 131104 | tf_op jit(solution)/shard_map/all_to_all | solution.py:207
  102.5 3.6 %all-to-all-start.2 = ((f32[8,64,128]{2,1,0:T(8,128)}), f32[8,64,128]{2,1,0:T(8,128)S(1)}, u32[]{:S(2)}, u32[]{:S(2)}) async-start(f32[8,64,128]{2,1,0:T(8,128)} %broadcast_select_fusion.8), calls=%async_computation.2 | async-start | bytes 524288 | tf_op jit(solution)/shard_map/all_to_all | solution.py:128
  109.0 2.6 %fusion.108 = f32[4,512,64]{1,0,2:T(4,128)} fusion(f32[8,512,64]{1,2,0:T(8,128)S(1)} %fusion.105, s32[8]{0:T(128)} %copy-done.58), kind=kOutput, calls=%fused_computation.193 | convolution fusion | flops 12582944 | bytes 1572896 | tf_op jit(solution)/shard_map/while/body/ng,nkd->gkd/dot_general | solution.py:226
  114.4 1.9 gather_fusion.7
  116.4 1.7 broadcast_select_fusion.1
  124.2 79.4 %while.68 = (s32[]{:T(128)}, f32[4,512,64]{1,2,0:T(8,128)}, f32[4,512,64]{1,2,0:T(8,128)}, f32[4,512,64]{1,2,0:T(8,128)}, bf16[4,512,64]{2,1,0:T(8,128)(2,1)}, /...) while((s32[]{:T(128)}, f32[4,512,64]{1,2,0:T(8,128)}, ...), condition=%wide.region_24.29_spmd.clone, body=%wide.region_23.28_spmd.clone.sunk | while | flops 106577920 | bytes 6987169 | solution.py:195
  136.4 1.6 fusion.256
  142.4 1.6 fusion.260
  162.3 1.6 fusion.260
  196.0 1.6 fusion.256
  205.4 4.6 %all-to-all-start.4 = ((f32[8,1,128]{2,1,0:T(1,128)}), f32[8,1,128]{2,1,0:T(1,128)S(1)}, u32[]{:S(2)}, u32[]{:S(2)}) async-start(f32[8,1,128]{2,1,0:T(1,128)} %bitcast.49), calls=%async_computation.4 | async-start | bytes 8192 | tf_op jit(solution)/shard_map/all_to_all | solution.py:208
  212.3 1.8 copy.186
  214.1 2.3 all-to-all-done.4
  217.2 2.0 multiply_convert_fusion
  222.8 2.4 while.66
  227.5 3.4 %all-to-all-start.5 = ((bf16[8,64,128]{2,1,0:T(8,128)(2,1)}), bf16[8,64,128]{2,1,0:T(8,128)(2,1)S(1)}, u32[]{:S(2)}, u32[]{:S(2)}) async-start(bf16[8,64,128]{2,1,0:T(8,128)(2,1)} %select_convert_fusion), calls=%async_computation.5 | async-start | bytes 262144 | tf_op jit(solution)/shard_map/all_to_all | solution.py:233
  233.8 4.4 %all-to-all-done.5 = bf16[8,64,128]{2,1,0:T(8,128)(2,1)S(1)} async-done(((bf16[8,64,128]{2,1,0:T(8,128)(2,1)}), bf16[8,64,128]{2,1,0:T(8,128)(2,1)S(1)}, u32[]{:S(2)}, u32[]{:S(2)}) %all-to-all-start.5) | async-done | bytes 131104 | tf_op jit(solution)/shard_map/all_to_all | solution.py:233
  (425 shorter events, 147.0 us)
Async XLA Ops:
  0.6 47.4 %copy-start.18 = (bf16[512,256]{1,0:T(8,128)(2,1)S(1)}, bf16[512,256]{1,0:T(8,128)(2,1)}, u32[]{:S(2)}) copy-start(bf16[512,256]{1,0:T(8,128)(2,1)} %param.21) | copy-start | bytes 786436
  0.7 49.6 %copy-start.21 = (bf16[512,256]{1,0:T(8,128)(2,1)S(1)}, bf16[512,256]{1,0:T(8,128)(2,1)}, u32[]{:S(2)}) copy-start(bf16[512,256]{1,0:T(8,128)(2,1)} %param.22) | copy-start | bytes 786436
  3.0 47.5 %copy-start.54 = (pred[4,4,3]{0,2,1:T(4,128)(4,1)}, pred[4,4,3]{0,2,1:T(4,128)(4,1)S(1)}, u32[]{:S(2)}) copy-start(pred[4,4,3]{0,2,1:T(4,128)(4,1)S(1)} %copy.157) | copy-start | bytes 148
  3.1 41.2 %copy-start.40 = (s32[4,4,3]{0,2,1:T(4,128)}, s32[4,4,3]{0,2,1:T(4,128)S(1)}, u32[]{:S(2)}) copy-start(s32[4,4,3]{0,2,1:T(4,128)S(1)} %copy.156) | copy-start | bytes 580
  3.1 47.4 %copy-start.22 = (bf16[512,256]{1,0:T(8,128)(2,1)S(1)}, bf16[512,256]{1,0:T(8,128)(2,1)}, u32[]{:S(2)}) copy-start(bf16[512,256]{1,0:T(8,128)(2,1)} %param.23) | copy-start | bytes 786436
  5.9 64.8 %all-to-all-start = ((bf16[8,64,128]{2,1,0:T(8,128)(2,1)}), bf16[8,64,128]{2,1,0:T(8,128)(2,1)S(1)}, u32[]{:S(2)}, u32[]{:S(2)}) async-start(bf16[8,64,128]{2,1,0:T(8,128)(2,1)} %copy.160), calls=%async_computation | async-start | bytes 262144 | tf_op jit(solution)/shard_map/all_to_all | solution.py:77
  50.3 21.1 %copy-start.44 = (pred[8]{0:T(512)(128)(4,1)}, pred[8]{0:T(512)(128)(4,1)S(1)}, u32[]{:S(2)}) copy-start(pred[8]{0:T(512)(128)(4,1)S(1)} %get-tuple-element.960) | copy-start | bytes 28
  74.1 15.2 %copy-start.31 = (pred[4,4,3]{2,1,0:T(4,128)(4,1)S(1)}, pred[4,4,3]{2,1,0:T(4,128)(4,1)}, u32[]{:S(2)}) copy-start(pred[4,4,3]{2,1,0:T(4,128)(4,1)} %get-tuple-element.956) | copy-start | bytes 148
  78.0 10.6 %all-to-all-start.1 = ((f32[8,1,128]{2,1,0:T(1,128)}), f32[8,1,128]{2,1,0:T(1,128)S(1)}, u32[]{:S(2)}, u32[]{:S(2)}) async-start(f32[8,1,128]{2,1,0:T(1,128)} %bitcast.19), calls=%async_computation.1 | async-start | bytes 8192 | tf_op jit(solution)/shard_map/all_to_all | solution.py:131
  83.9 23.7 %copy-start.20 = (f32[8,128]{1,0:T(8,128)S(1)}, f32[8,128]{1,0:T(8,128)}, u32[]{:S(2)}) copy-start(f32[8,128]{1,0:T(8,128)} %get-tuple-element.612) | copy-start | bytes 12292
  89.4 16.8 %copy-start.16 = (f32[4,4,3,128]{3,2,1,0:T(4,128)}, f32[4,4,3,128]{3,2,1,0:T(4,128)S(1)}, u32[]{:S(2)}) copy-start(f32[4,4,3,128]{3,2,1,0:T(4,128)S(1)} %gather.29) | copy-start | bytes 73732
  89.5 16.7 %copy-start.23 = (f32[4,4,128]{2,1,0:T(4,128)}, f32[4,4,128]{2,1,0:T(4,128)S(1)}, u32[]{:S(2)}) copy-start(f32[4,4,128]{2,1,0:T(4,128)S(1)} %fusion.126) | copy-start | bytes 24580
  89.7 16.5 %copy-start.28 = (f32[4,4,128]{2,1,0:T(4,128)}, f32[4,4,128]{2,1,0:T(4,128)S(1)}, u32[]{:S(2)}) copy-start(f32[4,4,128]{2,1,0:T(4,128)S(1)} %exponential_reduce_fusion.5) | copy-start | bytes 24580
  89.7 16.5 %copy-start.26 = (f32[4,4,128]{2,1,0:T(4,128)}, f32[4,4,128]{2,1,0:T(4,128)S(1)}, u32[]{:S(2)}) copy-start(f32[4,4,128]{2,1,0:T(4,128)S(1)} %get-tuple-element.955) | copy-start | bytes 24580
  91.1 11.4 %all-to-all-start.3 = ((bf16[8,64,128]{2,1,0:T(8,128)(2,1)}), bf16[8,64,128]{2,1,0:T(8,128)(2,1)S(1)}, u32[]{:S(2)}, u32[]{:S(2)}) async-start(bf16[8,64,128]{2,1,0:T(8,128)(2,1)} %copy.173), calls=%async_computation.3 | async-start | bytes 262144 | tf_op jit(solution)/shard_map/all_to_all | solution.py:207
  102.5 11.9 %all-to-all-start.2 = ((f32[8,64,128]{2,1,0:T(8,128)}), f32[8,64,128]{2,1,0:T(8,128)S(1)}, u32[]{:S(2)}, u32[]{:S(2)}) async-start(f32[8,64,128]{2,1,0:T(8,128)} %broadcast_select_fusion.8), calls=%async_computation.2 | async-start | bytes 524288 | tf_op jit(solution)/shard_map/all_to_all | solution.py:128
  124.2 79.5 %copy-start.17 = (f32[4,4,3,128]{3,2,1,0:T(4,128)S(1)}, f32[4,4,3,128]{3,2,1,0:T(4,128)}, u32[]{:S(2)}) copy-start(f32[4,4,3,128]{3,2,1,0:T(4,128)} %copy-done.16) | copy-start | bytes 73732
  124.2 79.5 %copy-start.27 = (f32[4,4,128]{2,1,0:T(4,128)S(1)}, f32[4,4,128]{2,1,0:T(4,128)}, u32[]{:S(2)}) copy-start(f32[4,4,128]{2,1,0:T(4,128)} %copy-done.26) | copy-start | bytes 24580
  124.2 79.5 %copy-start.32 = (pred[4,4,3]{2,1,0:T(4,128)(4,1)S(1)}, pred[4,4,3]{2,1,0:T(4,128)(4,1)}, u32[]{:S(2)}) copy-start(pred[4,4,3]{2,1,0:T(4,128)(4,1)} %get-tuple-element.956) | copy-start | bytes 148
  124.2 79.5 %copy-start.43 = (f32[4,4,128]{2,1,0:T(4,128)S(1)}, f32[4,4,128]{2,1,0:T(4,128)}, u32[]{:S(2)}) copy-start(f32[4,4,128]{2,1,0:T(4,128)} %copy.166) | copy-start | bytes 24580
  124.2 79.6 %copy-start.42 = (s32[4,4,3]{0,2,1:T(4,128)S(1)}, s32[4,4,3]{0,2,1:T(4,128)}, u32[]{:S(2)}) copy-start(s32[4,4,3]{0,2,1:T(4,128)} %copy-done.40) | copy-start | bytes 580
  124.2 85.8 %copy-start.38 = (f32[4,128,4]{1,0,2:T(4,128)S(1)}, f32[4,128,4]{1,0,2:T(4,128)}, u32[]{:S(2)}) copy-start(f32[4,128,4]{1,0,2:T(4,128)} %copy.162) | copy-start | bytes 24580
  205.4 11.1 %all-to-all-start.4 = ((f32[8,1,128]{2,1,0:T(1,128)}), f32[8,1,128]{2,1,0:T(1,128)S(1)}, u32[]{:S(2)}, u32[]{:S(2)}) async-start(f32[8,1,128]{2,1,0:T(1,128)} %bitcast.49), calls=%async_computation.4 | async-start | bytes 8192 | tf_op jit(solution)/shard_map/all_to_all | solution.py:208
  227.5 10.7 %all-to-all-start.5 = ((bf16[8,64,128]{2,1,0:T(8,128)(2,1)}), bf16[8,64,128]{2,1,0:T(8,128)(2,1)S(1)}, u32[]{:S(2)}, u32[]{:S(2)}) async-start(bf16[8,64,128]{2,1,0:T(8,128)(2,1)} %select_convert_fusion), calls=%async_computation.5 | async-start | bytes 262144 | tf_op jit(solution)/shard_map/all_to_all | solution.py:233
  (55 other events, 295.0 us)
where the time goes:
time: 246 us; the launch traced here: 241 us
  matrix products  92.1 us (37%)
  local copies, waits for them, and re-layouts  43.3 us (18%)
  blocking collectives  31.1 us (13%)
  other arithmetic  27.1 us (11%)
  starting transfers between devices  26.5 us (11%)
  waiting for transfers between devices  18.2 us (7%)
    all_gather x1, blocking collectives, local(): all_picks = lax.all_gather(picks, 'ctx', axis=0, tiled=True)  31.1 us
    dot_general x16, matrix products, own_backward(): jnp.einsum('qk,qd->kd', dscore, q_part, preferred_element_type=jnp.float32)  18 us
    dot_general x16, matrix products, own_backward(): jnp.einsum('qk,qd->kd', attend_low, g_part, preferred_element_type=jnp.fl...  18 us
    dot_general x16, matrix products, own_backward(): jnp.einsum('qd,kd->qk', g_part, v_head[:span], preferred_element_type=jnp...  16.9 us
    dot_general x16, matrix products, own_backward(): jnp.einsum('qd,kd->qk', q_part, k_part, preferred_element_type=jnp.float32)  16.4 us
    unnamed x127, local copies, waits for them, and re-layouts  9.96 us
    all_to_all x1, starting transfers between devices, local(): lax.all_to_all(send_q, 'ctx', split_axis=0, concat_axis=0, tiled=True)  7.28 us
    all_to_all x1, waiting for transfers between devices, local(): lax.all_to_all(send_g, 'ctx', split_axis=0, concat_axis=0, tiled=True)  6.1 us
  transfers between devices with their start and end apart: 6, of which 5 were waited for; matrix products, arithmetic and copies ran while one was open for 18% of the time, Pallas kernels for 0%

commit v1 on v0

--- a/solution.py
+++ b/solution.py
@@ -3,10 +3,14 @@
 import jax
 import jax.numpy as jnp
 from jax import lax
+from jax.experimental import pallas as pl
+from jax.experimental.pallas import tpu as pltpu
 from jax.sharding import PartitionSpec as P
 
 masked_value = -1e30
 highest = lax.Precision.HIGHEST
+LOG2E = math.log2(math.e)
+pair_budget = 8 << 20
 
 
 def attend_slots(q_slots, head_ids, k_heads, v_heads, scaling):
@@ -251,6 +255,393 @@
     return (attn_out, grad_query, grad_key, grad_value)
 
 
+def pack_kernel(tiles_dev, groups, picked, tile_rows, head_dim, devices):
+    def body(picks_ref, q_ref, g_ref, send_ref, task_ref):
+        own = picks_ref[0, 0, 0]
+        meta_rows = send_ref.shape[1] - tile_rows
+        lanes = send_ref.shape[2]
+        row = lax.broadcasted_iota(jnp.int32, (meta_rows, lanes), 0)
+        blank = jnp.zeros((meta_rows, lanes), jnp.bfloat16)
+        for peer in range(devices):
+            send_ref[peer, tile_rows:, :] = blank
+            task_ref[peer] = -1
+        for tile in range(tiles_dev):
+            rows = slice(tile * tile_rows, (tile + 1) * tile_rows)
+            for head in range(groups):
+                cols = slice(head * head_dim, (head + 1) * head_dim)
+                block = jnp.concatenate([q_ref[rows, cols], g_ref[rows, cols]], axis=1)
+                code = tile * groups + head
+                meta = jnp.where(row == 0, code + 1, 0)
+                for entry in range(1, picked):
+                    meta = jnp.where(row == entry, picks_ref[tile, head, entry], meta)
+                meta = meta.astype(jnp.float32).astype(jnp.bfloat16)
+                for entry in range(1, picked):
+                    target = picks_ref[tile, head, entry]
+                    send_ref[target, :tile_rows, :] = block
+                    send_ref[target, tile_rows:, :] = meta
+                    task_ref[target] = code
+        task_ref[own] = -1
+
+    return body
+
+
+def soft_parts(scores, grads):
+    peak = jnp.max(scores, axis=0, keepdims=True)
+    powers = jnp.exp2(scores - peak)
+    total = jnp.sum(powers, axis=0, keepdims=True)
+    inverse = 1.0 / total
+    mean_grad = jnp.sum(powers * grads, axis=0, keepdims=True) * inverse
+    spread = powers * (grads - mean_grad)
+    both = jnp.concatenate([powers.astype(jnp.bfloat16), spread.astype(jnp.bfloat16)], axis=1)
+    return both, peak + jnp.log2(total), mean_grad, inverse
+
+
+def split_low(x):
+    high = x.astype(jnp.bfloat16).astype(jnp.float32)
+    return high, x - high
+
+
+def paired(block, head_dim):
+    lane = lax.broadcasted_iota(jnp.int32, block.shape, 1)
+    zero = jnp.zeros_like(block)
+    left = jnp.where(lane < head_dim, block, zero)
+    right = jnp.where(lane < head_dim, zero, block)
+    return jnp.concatenate([left, right], axis=0)
+
+
+def dot_t(a, b):
+    return lax.dot_general(a, b, (((1,), (1,)), ((), ())), preferred_element_type=jnp.float32)
+
+
+def own_kernel(tiles_dev, groups, tile_rows, head_dim, devices):
+    scale = LOG2E / math.sqrt(head_dim)
+
+    def body(q_ref, k_ref, v_ref, g_ref, kv_ref, vkt_ref, qgt_ref, mix_ref, dot_ref, stat_ref,
+             table_ref, *pd_refs):
+        sub = lax.broadcasted_iota(jnp.int32, (tile_rows, tile_rows), 0)
+        lane = lax.broadcasted_iota(jnp.int32, (tile_rows, tile_rows), 1)
+        causal = sub <= lane
+        for head in range(groups):
+            cols = slice(head * head_dim, (head + 1) * head_dim)
+            k_head = k_ref[:, cols]
+            v_head = v_ref[:, cols]
+            kv_ref[head] = jnp.concatenate([k_head, v_head], axis=1)
+            vkt_ref[head] = jnp.concatenate([v_head, k_head], axis=1).T
+            qgt_ref[head] = jnp.concatenate([q_ref[:, cols], g_ref[:, cols]], axis=1).T
+            for tile in range(tiles_dev):
+                rows = slice(tile * tile_rows, (tile + 1) * tile_rows)
+                span = (tile + 1) * tile_rows
+                code = tile * groups + head
+                block = jnp.concatenate([q_ref[rows, cols], g_ref[rows, cols]], axis=1)
+                both = dot_t(kv_ref[head, :span, :], paired(block, head_dim))
+                scores = both[:, :tile_rows] * scale
+                last = jnp.where(causal, scores[span - tile_rows :], masked_value)
+                if tile:
+                    scores = jnp.concatenate([scores[: span - tile_rows], last], axis=0)
+                else:
+                    scores = last
+                pair, lse, mean_grad, inverse = soft_parts(scores, both[:, tile_rows:])
+                for part in range(tile + 1):
+                    pd_refs[part][head, :, (tile - part) * 2 * tile_rows : (tile - part + 1) * 2 * tile_rows] = (
+                        pair[part * tile_rows : (part + 1) * tile_rows]
+                    )
+                result = jnp.dot(vkt_ref[head, :, :span], pair, preferred_element_type=jnp.float32)
+                mix_ref[code] = result[:, :tile_rows] * inverse
+                dot_ref[code] = result[head_dim:, tile_rows:] * inverse
+                stat_ref[0, code : code + 1, :] = lse
+                stat_ref[1, code : code + 1, :] = mean_grad
+                stat_ref[2, code : code + 1, :] = inverse
+                parts = split_low(lse) + split_low(mean_grad)
+                table_ref[code] = jnp.concatenate(
+                    [jnp.broadcast_to(p, (devices, tile_rows)) for p in parts], axis=0
+                )
+
+    return body
+
+
+def serve_kernel(groups, tile_rows, head_dim, devices):
+    scale = LOG2E / math.sqrt(head_dim)
+
+    def body(picks_ref, task_ref, recv_ref, kv_ref, vkt_ref, table_ref, send_ref, pd_ref, inv_ref, st_ref):
+        own = picks_ref[0, 0, 0]
+        st_ref[...] = jnp.zeros_like(st_ref)
+        inv_ref[...] = jnp.zeros_like(inv_ref)
+
+        def turn(source, carry):
+            code = jnp.max(recv_ref[source, tile_rows:, :].astype(jnp.float32)[0:1, :]).astype(jnp.int32) - 1
+
+            @pl.when(code >= 0)
+            def _():
+                head = lax.rem(code, groups)
+                block = recv_ref[source, :tile_rows, :]
+                both = dot_t(kv_ref[head], paired(block, head_dim))
+                pair, lse, mean_grad, inverse = soft_parts(both[:, :tile_rows] * scale, both[:, tile_rows:])
+                pd_ref[source] = pair
+                result = jnp.dot(vkt_ref[head], pair, preferred_element_type=jnp.float32)
+                send_ref[source, : 2 * head_dim, :] = (result[:, :tile_rows] * inverse).astype(jnp.bfloat16)
+                send_ref[source, 2 * head_dim : 3 * head_dim, :] = (
+                    result[head_dim:, tile_rows:] * inverse
+                ).astype(jnp.bfloat16)
+                parts = split_low(lse) + split_low(mean_grad)
+                for index in range(4):
+                    st_ref[pl.ds(index * devices + source, 1), :] = parts[index]
+                inv_ref[pl.ds(source, 1), :] = inverse
+
+            return carry
+
+        lax.fori_loop(own + 1, devices, turn, 0)
+        table = st_ref[...]
+        row = lax.broadcasted_iota(jnp.int32, table.shape, 0)
+        mine = lax.rem(row, devices) == own
+        for peer in range(devices):
+            code = jnp.maximum(task_ref[peer], 0)
+            send_ref[peer, 3 * head_dim :, :] = jnp.where(mine, table_ref[code], table).astype(jnp.bfloat16)
+
+    return body
+
+
+def flip_kernel(devices, tile_rows):
+    def body(recv_ref, qgt_ref):
+        for source in range(1, devices):
+            qgt_ref[source] = recv_ref[source, :tile_rows, :].T
+
+    return body
+
+
+def final_kernel(tiles_dev, groups, picked, tile_rows, head_dim, devices):
+    scaling = 1.0 / math.sqrt(head_dim)
+
+    def body(picks_ref, task_ref, recv_ref, back_ref, qgt_ref, qgt_in_ref, mix_ref, dot_ref, stat_ref,
+             inv_ref, pd_in_ref, *rest):
+        pd_refs = rest[:tiles_dev]
+        out_ref, dq_ref, dk_ref, dv_ref, acc_ref, grad_ref, lse_sc, gd_sc, w_sc, d_sc, x_ref = rest[tiles_dev:]
+        own = picks_ref[0, 0, 0]
+        tasks = tiles_dev * groups
+        base = 3 * head_dim
+
+        lse_of = []
+        gd_of = []
+        for peer in range(devices):
+            table = back_ref[peer, base : base + 4 * devices, :].astype(jnp.float32)
+            lse_of.append(table[:devices] + table[devices : 2 * devices])
+            gd_of.append(table[2 * devices : 3 * devices] + table[3 * devices :])
+            lse_sc[peer] = lse_of[peer]
+            gd_sc[peer] = gd_of[peer]
+
+        ids = lax.broadcasted_iota(jnp.int32, (devices, tile_rows), 0)
+        metas = [recv_ref[source, tile_rows : tile_rows + 16, :].astype(jnp.float32) for source in range(devices)]
+        lists = [
+            jnp.concatenate([metas[source][entry : entry + 1] for source in range(devices)], axis=0).astype(jnp.int32)
+            for entry in range(1, picked)
+        ]
+        chosen = []
+        for peer in range(devices):
+            active = ids == peer
+            for entry in lists:
+                active = active | (entry == peer)
+            chosen.append(active)
+        peak = jnp.full((devices, tile_rows), masked_value, jnp.float32)
+        for peer in range(devices):
+            peak = jnp.maximum(peak, jnp.where(chosen[peer], lse_of[peer], masked_value))
+        total = jnp.zeros_like(peak)
+        delta = jnp.zeros_like(peak)
+        for peer in range(devices):
+            power = jnp.where(chosen[peer], jnp.exp2(lse_of[peer] - peak), 0.0)
+            total = total + power
+            delta = delta + jnp.where(chosen[peer], power * gd_of[peer], 0.0)
+        delta = delta / total
+        mine_gd = gd_sc[own]
+        weight = jnp.exp2(lse_sc[own] - peak) / total * inv_ref[...]
+        w_sc[0] = weight
+        w_sc[1] = weight * (mine_gd - delta)
+
+        code_ids = lax.broadcasted_iota(jnp.int32, (tasks, tile_rows), 0)
+        own_lse = stat_ref[0]
+        own_gd = stat_ref[1]
+        peak = own_lse
+        rows_lse = [lse_sc[peer, pl.ds(own, 1), :] for peer in range(devices)]
+        rows_gd = [gd_sc[peer, pl.ds(own, 1), :] for peer in range(devices)]
+        for peer in range(devices):
+            peak = jnp.maximum(peak, jnp.where(code_ids == task_ref[peer], rows_lse[peer], masked_value))
+        own_power = jnp.exp2(own_lse - peak)
+        total = own_power
+        delta = own_power * own_gd
+        for peer in range(devices):
+            here = code_ids == task_ref[peer]
+            power = jnp.where(here, jnp.exp2(rows_lse[peer] - peak), 0.0)
+            total = total + power
+            delta = delta + jnp.where(here, power * rows_gd[peer], 0.0)
+        inverse = 1.0 / total
+        delta = delta * inverse
+        own_weight = own_power * inverse
+        d_sc[0] = peak
+        d_sc[1] = inverse
+        d_sc[2] = delta
+        d_sc[3] = own_weight
+        d_sc[4] = own_weight * stat_ref[2]
+        d_sc[5] = own_weight * stat_ref[2] * (own_gd - delta)
+        d_sc[6] = own_weight * (own_gd - delta)
+
+        for code in range(tasks):
+            mix = mix_ref[code]
+            acc_ref[code, :head_dim, :] = mix[:head_dim] * d_sc[3, code : code + 1, :]
+            acc_ref[code, head_dim:, :] = (
+                dot_ref[code] * d_sc[3, code : code + 1, :] + mix[head_dim:] * d_sc[6, code : code + 1, :]
+            )
+
+        def gather(peer, carry):
+            code = task_ref[peer]
+
+            @pl.when(code >= 0)
+            def _():
+                at = pl.ds(code, 1)
+                part_w = jnp.exp2(lse_sc[peer, pl.ds(own, 1), :] - d_sc[0, at, :]) * d_sc[1, at, :]
+                shift = part_w * (gd_sc[peer, pl.ds(own, 1), :] - d_sc[2, at, :])
+                mix = back_ref[peer, : 2 * head_dim, :].astype(jnp.float32)
+                low = back_ref[peer, 2 * head_dim : 3 * head_dim, :].astype(jnp.float32)
+                acc_ref[code, :head_dim, :] += mix[:head_dim] * part_w
+                acc_ref[code, head_dim:, :] += low * part_w + mix[head_dim:] * shift
+
+            return carry
+
+        lax.fori_loop(0, own, gather, 0)
+
+        for head in range(groups):
+            for tile in range(tiles_dev):
+                code = tile * groups + head
+                first = d_sc[4, code : code + 1, :]
+                second = d_sc[5, code : code + 1, :]
+                turned = qgt_ref[head, :, tile * tile_rows : (tile + 1) * tile_rows].astype(jnp.float32)
+                at = tile * 2 * tile_rows
+                x_ref[:head_dim, at : at + tile_rows] = (turned[head_dim:] * first).astype(jnp.bfloat16)
+                x_ref[:head_dim, at + tile_rows : at + 2 * tile_rows] = jnp.zeros((head_dim, tile_rows), jnp.bfloat16)
+                x_ref[head_dim:, at : at + tile_rows] = (turned[:head_dim] * second).astype(jnp.bfloat16)
+                x_ref[head_dim:, at + tile_rows : at + 2 * tile_rows] = (turned[:head_dim] * first).astype(jnp.bfloat16)
+            for part in range(tiles_dev):
+                grad_ref[head, part * tile_rows : (part + 1) * tile_rows, :] = dot_t(
+                    pd_refs[part][head], x_ref[:, part * 2 * tile_rows :]
+                )
+
+        def spread(source, carry):
+            code = jnp.max(recv_ref[source, tile_rows:, :].astype(jnp.float32)[0:1, :]).astype(jnp.int32) - 1
+
+            @pl.when(code >= 0)
+            def _():
+                head = lax.rem(code, groups)
+                first = w_sc[0, pl.ds(source, 1), :]
+                second = w_sc[1, pl.ds(source, 1), :]
+                turned = qgt_in_ref[source].astype(jnp.float32)
+                top = jnp.concatenate([turned[head_dim:] * first, jnp.zeros((head_dim, tile_rows), jnp.float32)], axis=1)
+                low = jnp.concatenate([turned[:head_dim] * second, turned[:head_dim] * first], axis=1)
+                factor = jnp.concatenate([top, low], axis=0).astype(jnp.bfloat16)
+                grad_ref[head] += dot_t(pd_in_ref[source], factor)
+
+            return carry
+
+        lax.fori_loop(own + 1, devices, spread, 0)
+
+        for head in range(groups):
+            cols = slice(head * head_dim, (head + 1) * head_dim)
+            dv_ref[:, cols] = grad_ref[head, :, :head_dim].astype(jnp.bfloat16)
+            dk_ref[:, cols] = (grad_ref[head, :, head_dim:] * scaling).astype(jnp.bfloat16)
+            for tile in range(tiles_dev):
+                rows = slice(tile * tile_rows, (tile + 1) * tile_rows)
+                turned = acc_ref[tile * groups + head].T
+                out_ref[rows, cols] = turned[:, :head_dim].astype(jnp.bfloat16)
+                dq_ref[rows, cols] = (turned[:, head_dim:] * scaling).astype(jnp.bfloat16)
+
+    return body
+
+
+def fast_local(query, key, value, grad_out, picks):
+    row_count, columns = query.shape
+    tiles_dev, groups, picked = picks.shape
+    head_dim = columns // groups
+    tile_rows = row_count // tiles_dev
+    devices = lax.axis_size("ctx")
+    tasks = tiles_dev * groups
+    smem = pl.BlockSpec(memory_space=pltpu.SMEM)
+    vmem = pl.BlockSpec(memory_space=pltpu.VMEM)
+    low = jnp.bfloat16
+    wide = jnp.float32
+    width = 2 * head_dim
+    shape = jax.ShapeDtypeStruct
+
+    send_q, task_of = pl.pallas_call(
+        pack_kernel(tiles_dev, groups, picked, tile_rows, head_dim, devices),
+        out_shape=(shape((devices, tile_rows + 16, width), low), shape((devices,), jnp.int32)),
+        in_specs=[smem, vmem, vmem],
+        out_specs=(vmem, smem),
+        name="pack",
+    )(picks, query, grad_out)
+    recv_q = lax.all_to_all(send_q, "ctx", split_axis=0, concat_axis=0, tiled=True)
+
+    own_shapes = (
+        shape((groups, row_count, width), low),
+        shape((groups, width, row_count), low),
+        shape((groups, width, row_count), low),
+        shape((tasks, width, tile_rows), wide),
+        shape((tasks, head_dim, tile_rows), wide),
+        shape((3, tasks, tile_rows), wide),
+        shape((tasks, 4 * devices, tile_rows), wide),
+    ) + tuple(
+        shape((groups, tile_rows, (tiles_dev - part) * 2 * tile_rows), low) for part in range(tiles_dev)
+    )
+    kv, vkt, qgt, mix, dots, stats, table, *pairs = pl.pallas_call(
+        own_kernel(tiles_dev, groups, tile_rows, head_dim, devices),
+        out_shape=own_shapes,
+        in_specs=[vmem] * 4,
+        out_specs=tuple([vmem] * len(own_shapes)),
+        name="own",
+    )(query, key, value, grad_out)
+
+    slot = 3 * head_dim + 4 * devices
+    send_b, pairs_in, inverse_in = pl.pallas_call(
+        serve_kernel(groups, tile_rows, head_dim, devices),
+        out_shape=(
+            shape((devices, slot, tile_rows), low),
+            shape((devices, row_count, 2 * tile_rows), low),
+            shape((devices, tile_rows), wide),
+        ),
+        in_specs=[smem, smem, vmem, vmem, vmem, vmem],
+        out_specs=(vmem, vmem, vmem),
+        scratch_shapes=[pltpu.VMEM((4 * devices, tile_rows), wide)],
+        name="serve",
+    )(picks, task_of, recv_q, kv, vkt, table)
+    recv_b = lax.all_to_all(send_b, "ctx", split_axis=0, concat_axis=0, tiled=True)
+
+    qgt_in = pl.pallas_call(
+        flip_kernel(devices, tile_rows),
+        out_shape=shape((devices, width, tile_rows), low),
+        in_specs=[vmem],
+        out_specs=vmem,
+        name="flip",
+    )(recv_q)
+
+    return pl.pallas_call(
+        final_kernel(tiles_dev, groups, picked, tile_rows, head_dim, devices),
+        out_shape=tuple([shape((row_count, columns), low)] * 4),
+        in_specs=[smem, smem] + [vmem] * (9 + tiles_dev),
+        out_specs=tuple([vmem] * 4),
+        scratch_shapes=[
+            pltpu.VMEM((tasks, width, tile_rows), wide),
+            pltpu.VMEM((groups, row_count, width), wide),
+            pltpu.VMEM((devices, devices, tile_rows), wide),
+            pltpu.VMEM((devices, devices, tile_rows), wide),
+            pltpu.VMEM((2, devices, tile_rows), wide),
+            pltpu.VMEM((7, tasks, tile_rows), wide),
+            pltpu.VMEM((width, 2 * row_count), low),
+        ],
+        name="final",
+    )(picks, task_of, recv_q, recv_b, qgt, qgt_in, mix, dots, stats, inverse_in, pairs_in, *pairs)
+
+
+def choose(query, key, value, grad_out, picks):
+    pair_bytes = lax.axis_size("ctx") * query.shape[0] * (query.shape[0] // picks.shape[0]) * 4
+    plan = fast_local if pair_bytes <= pair_budget else local
+    return plan(query, key, value, grad_out, picks)
+
+
 def solution(mesh):
     placed = (
         P("ctx", "head"),
@@ -260,7 +651,7 @@
         P("ctx", "head", None),
     )
     return jax.shard_map(
-        local,
+        choose,
         mesh=mesh,
         in_specs=placed,
         out_specs=(P("ctx", "head"), P("ctx", "head"), P("ctx", "head"), P("ctx", "head")),

time: 246 us -> 53.6 us (0.22); the launches traced: 241 us -> 53.2 us
  matrix products: 92.1 us -> 0 us
  local copies, waits for them, and re-layouts: 43.3 us -> 1.53 us
  blocking collectives: 31.1 us -> 0 us
  Pallas kernels: 0 us -> 29 us
  other arithmetic: 27.1 us -> 0 us
  starting transfers between devices: 26.5 us -> 10.8 us
  waiting for transfers between devices: 18.2 us -> 11.2 us
    dot_general x123 -> x0, matrix products: 92.1 us -> none  [the longest x16 18 us: own_backward(): jnp.einsum('qk,qd->kd', dscore, q_part, preferred_element_type=jnp.float32)]
    all_gather x1 -> x0, blocking collectives: 31.1 us -> none  [local(): all_picks = lax.all_gather(picks, 'ctx', axis=0, tiled=True)]
    pallas_call x0 -> x5, Pallas kernels: none -> 29 us  [the longest x1 8.46 us: fast_local(): pl.pallas_call(final_kernel(tiles_dev, groups, picked, tile_rows, head_di...]
    all_to_all x6 -> x2, starting transfers between devices: 26.5 us -> 10.8 us  [the longest x1 7.29 us: fast_local(): lax.all_to_all(send_q, 'ctx', split_axis=0, concat_axis=0, tiled=True)]
    gather x13 -> x0, local copies, waits for them, and re-layouts: 11.6 us -> none  [the longest x1 1.95 us: local(): jnp.take(back_out, lookup, axis=0)]
    unnamed x127 -> x4, local copies, waits for them, and re-layouts: 9.96 us -> 1.53 us
    all_to_all x6 -> x2, waiting for transfers between devices: 18.2 us -> 11.2 us  [the longest x1 10 us: fast_local(): lax.all_to_all(send_b, 'ctx', split_axis=0, concat_axis=0, tiled=True)]
    while x38 -> x0, local copies, waits for them, and re-layouts: 4.69 us -> none  [the longest x4 3.35 us: local(): lax.fori_loop(0, rounds, backward_turn, start_bwd)]
  transfers between devices with their start and end apart: 6 -> 2, of which waited for: 5 -> 2; matrix products, arithmetic and copies ran while one was open for 18% -> 0% of each run, Pallas kernels for 0% -> 19%
where the time goes in v1:
time: 53.6 us; the launch traced here: 53.2 us
  Pallas kernels  29 us (54%)
  waiting for transfers between devices  11.2 us (21%)
  starting transfers between devices  10.8 us (20%)
  local copies, waits for them, and re-layouts  1.53 us (3%)
  between operations  0.65 us (1%)
    all_to_all x1, waiting for transfers between devices, fast_local(): lax.all_to_all(send_b, 'ctx', split_axis=0, concat_axis=0, tiled=True)  10 us
    pallas_call x1, Pallas kernels, fast_local(): pl.pallas_call(final_kernel(tiles_dev, groups, picked, tile_rows, head_di...  8.46 us
    pallas_call x1, Pallas kernels, fast_local(): pl.pallas_call(own_kernel(tiles_dev, groups, tile_rows, head_dim, devices...  8.43 us
    pallas_call x1, Pallas kernels, fast_local(): pl.pallas_call(serve_kernel(groups, tile_rows, head_dim, devices), out_sh...  8.2 us
    all_to_all x1, starting transfers between devices, fast_local(): lax.all_to_all(send_q, 'ctx', split_axis=0, concat_axis=0, tiled=True)  7.29 us
    all_to_all x1, starting transfers between devices, fast_local(): lax.all_to_all(send_b, 'ctx', split_axis=0, concat_axis=0, tiled=True)  3.47 us
    pallas_call x1, Pallas kernels, fast_local(): pl.pallas_call(pack_kernel(tiles_dev, groups, picked, tile_rows, head_dim...  2.1 us
    pallas_call x1, Pallas kernels, fast_local(): pl.pallas_call(flip_kernel(devices, tile_rows), out_shape=shape((devices,...  1.8 us
  transfers between devices with their start and end apart: 2, of which 2 were waited for; matrix products, arithmetic and copies ran while one was open for 0% of the time, Pallas kernels for 19%

profile of v1, /device:TPU:0, one launch (start us, length us, event | category | flops | bytes accessed | tf_op | source)
XLA Modules:
  0.0 53.2 jit_solution(5775864518471197118)
XLA Ops:
  0.6 2.1 %pack.1 = (bf16[8,144,128]{2,1,0:T(8,128)(2,1)}, s32[8]{0:T(128)}) custom-call(s32[4,4,4]{2,1,0:T(4,128)} %picks_ref.5, bf16[512,256]{1,0:T(8,128)(2,1)} %q_ref.3, bf16[512,256]{1,0:T(8,128)(2,1)} %g_ref.3), custom_call_target="tpu_custom_call" | custom-call | tf_op jit(solution)/shard_map/pack/pallas_call | solution.py:570
  2.7 7.3 %all-to-all-start = ((bf16[8,144,128]{2,1,0:T(8,128)(2,1)}), bf16[8,144,128]{2,1,0:T(8,128)(2,1)S(1)}, u32[]{:S(2)}, u32[]{:S(2)}) async-start(bf16[8,144,128]{2,1,0:T(8,128)(2,1)} %get-tuple-element.21), calls=%async_computation | async-start | bytes 589824 | tf_op jit(solution)/shard_map/all_to_all | solution.py:577
  10.0 8.4 %own.1 = (bf16[4,512,128]{2,1,0:T(8,128)(2,1)}, bf16[4,128,512]{2,1,0:T(8,128)(2,1)}, bf16[4,128,512]{2,1,0:T(8,128)(2,1)}, f32[16,128,128]{2,1,0:T(8,128)}, f32...) custom-call(bf16[512,256]{1,0:T(8,128)(2,1)} %q_ref.3, ...), custom_call_target="tpu_custom_call" | custom-call | tf_op jit(solution)/shard_map/own/pallas_call | solution.py:590
  18.5 1.2 %all-to-all-done.recv_ref = bf16[8,144,128]{2,1,0:T(8,128)(2,1)S(1)} async-done(((bf16[8,144,128]{2,1,0:T(8,128)(2,1)}), bf16[8,144,128]{2,1,0:T(8,128)(2,1)S(1)}, u32[]{:S(2)}, u32[]{:S(2)}) %all-to-all-start) | async-done | bytes 294944 | tf_op jit(solution)/shard_map/all_to_all | solution.py:577
  19.6 0.0 copy-start
  19.6 0.8 %copy-done = bf16[8,144,128]{2,1,0:T(8,128)(2,1)} copy-done((bf16[8,144,128]{2,1,0:T(8,128)(2,1)}, bf16[8,144,128]{2,1,0:T(8,128)(2,1)S(1)}, u32[]{:S(2)}) %copy-start) | copy-done | bytes 294936
  20.4 8.2 %serve.1 = (bf16[8,224,128]{2,1,0:T(8,128)(2,1)}, bf16[8,512,256]{2,1,0:T(8,128)(2,1)}, f32[8,128]{1,0:T(8,128)}) custom-call(s32[4,4,4]{2,1,0:T(4,128)} %picks_ref.5, s32[8]{0:T(128)} %get-tuple-element.20.task_ref, bf16[8,144,128]{2,1,0:T(8,128)(2,1)} %copy-done, bf16[4,512,128]{2,1,0:T(8,128)(2,1)} %get-tuple-element.22.kv_ref, ...), custom_call_target="tpu_custom_call" | custom-call | tf_op jit(solution)/shard_map/serve/pallas_call | solution.py:599
  28.6 3.5 %all-to-all-start.1 = ((bf16[8,224,128]{2,1,0:T(8,128)(2,1)}), bf16[8,224,128]{2,1,0:T(8,128)(2,1)S(1)}, u32[]{:S(2)}, u32[]{:S(2)}) async-start(bf16[8,224,128]{2,1,0:T(8,128)(2,1)} %get-tuple-element.25), calls=%async_computation.1 | async-start | bytes 917504 | tf_op jit(solution)/shard_map/all_to_all | solution.py:611
  32.1 1.8 %flip.1.qgt_in_ref = bf16[8,128,128]{2,1,0:T(8,128)(2,1)} custom-call(bf16[8,144,128]{2,1,0:T(8,128)(2,1)} %copy-done), custom_call_target="tpu_custom_call" | custom-call | tf_op jit(solution)/shard_map/flip/pallas_call | solution.py:613
  33.9 10.0 %all-to-all-done.1.back_ref = bf16[8,224,128]{2,1,0:T(8,128)(2,1)S(1)} async-done(((bf16[8,224,128]{2,1,0:T(8,128)(2,1)}), bf16[8,224,128]{2,1,0:T(8,128)(2,1)S(1)}, u32[]{:S(2)}, u32[]{:S(2)}) %all-to-all-start.1) | async-done | bytes 458784 | tf_op jit(solution)/shard_map/all_to_all | solution.py:611
  43.9 0.0 copy-start.1
  43.9 0.8 %copy-done.1 = bf16[8,224,128]{2,1,0:T(8,128)(2,1)} copy-done((bf16[8,224,128]{2,1,0:T(8,128)(2,1)}, bf16[8,224,128]{2,1,0:T(8,128)(2,1)S(1)}, u32[]{:S(2)}) %copy-start.1) | copy-done | bytes 458776
  44.7 8.5 %final.1 = (bf16[512,256]{1,0:T(8,128)(2,1)}, bf16[512,256]{1,0:T(8,128)(2,1)}, bf16[512,256]{1,0:T(8,128)(2,1)}, bf16[512,256]{1,0:T(8,128)(2,1)}) custom-call(s32[4,4,4]{2,1,0:T(4,128)} %picks_ref.5, s32[8]{0:T(128)} %get-tuple-element.20.task_ref, bf16[8,144,128]{2,1,0:T(8,128)(2,1)} %copy-done, bf16[8,224,128]{2,1,0:T(8,128)(2,1)} %copy-done.1, ...), custom_call_target="tpu_custom_call" | custom-call | tf_op jit(solution)/shard_map/final/pallas_call | solution.py:621
Async XLA Ops:
  2.7 16.9 %all-to-all-start = ((bf16[8,144,128]{2,1,0:T(8,128)(2,1)}), bf16[8,144,128]{2,1,0:T(8,128)(2,1)S(1)}, u32[]{:S(2)}, u32[]{:S(2)}) async-start(bf16[8,144,128]{2,1,0:T(8,128)(2,1)} %get-tuple-element.21), calls=%async_computation | async-start | bytes 589824 | tf_op jit(solution)/shard_map/all_to_all | solution.py:577
  19.6 0.8 %copy-start = (bf16[8,144,128]{2,1,0:T(8,128)(2,1)}, bf16[8,144,128]{2,1,0:T(8,128)(2,1)S(1)}, u32[]{:S(2)}) copy-start(bf16[8,144,128]{2,1,0:T(8,128)(2,1)S(1)} %all-to-all-done.recv_ref) | copy-start | bytes 884740
  28.6 15.3 %all-to-all-start.1 = ((bf16[8,224,128]{2,1,0:T(8,128)(2,1)}), bf16[8,224,128]{2,1,0:T(8,128)(2,1)S(1)}, u32[]{:S(2)}, u32[]{:S(2)}) async-start(bf16[8,224,128]{2,1,0:T(8,128)(2,1)} %get-tuple-element.25), calls=%async_computation.1 | async-start | bytes 917504 | tf_op jit(solution)/shard_map/all_to_all | solution.py:611
  43.9 0.8 %copy-start.1 = (bf16[8,224,128]{2,1,0:T(8,128)(2,1)}, bf16[8,224,128]{2,1,0:T(8,128)(2,1)S(1)}, u32[]{:S(2)}) copy-start(bf16[8,224,128]{2,1,0:T(8,128)(2,1)S(1)} %all-to-all-done.1.back_ref) | copy-start | bytes 1376260

commit v2 on v1

--- a/solution.py
+++ b/solution.py
@@ -11,6 +11,8 @@
 highest = lax.Precision.HIGHEST
 LOG2E = math.log2(math.e)
 pair_budget = 8 << 20
+vmem_grant = 57 << 20
+vmem_whole = 65400 << 10
 
 
 def attend_slots(q_slots, head_ids, k_heads, v_heads, scaling):
@@ -255,6 +257,28 @@
     return (attn_out, grad_query, grad_key, grad_value)
 
 
+def offsets_of(tiles_dev, tile_rows):
+    starts = [0]
+    for part in range(tiles_dev):
+        starts.append(starts[-1] + (tiles_dev - part) * 2 * tile_rows)
+    return starts
+
+
+def dot_t(a, b):
+    return lax.dot_general(a, b, (((1,), (1,)), ((), ())), preferred_element_type=jnp.float32)
+
+
+def split_low(x):
+    high = x.astype(jnp.bfloat16).astype(jnp.float32)
+    return high, x - high
+
+
+def halves(block, head_dim):
+    lane = lax.broadcasted_iota(jnp.int32, block.shape, 1)
+    zero = jnp.zeros_like(block)
+    return jnp.where(lane < head_dim, block, zero), jnp.where(lane < head_dim, zero, block)
+
+
 def pack_kernel(tiles_dev, groups, picked, tile_rows, head_dim, devices):
     def body(picks_ref, q_ref, g_ref, send_ref, task_ref):
         own = picks_ref[0, 0, 0]
@@ -285,69 +309,69 @@
     return body
 
 
-def soft_parts(scores, grads):
-    peak = jnp.max(scores, axis=0, keepdims=True)
-    powers = jnp.exp2(scores - peak)
-    total = jnp.sum(powers, axis=0, keepdims=True)
-    inverse = 1.0 / total
-    mean_grad = jnp.sum(powers * grads, axis=0, keepdims=True) * inverse
-    spread = powers * (grads - mean_grad)
-    both = jnp.concatenate([powers.astype(jnp.bfloat16), spread.astype(jnp.bfloat16)], axis=1)
-    return both, peak + jnp.log2(total), mean_grad, inverse
-
-
-def split_low(x):
-    high = x.astype(jnp.bfloat16).astype(jnp.float32)
-    return high, x - high
-
-
-def paired(block, head_dim):
-    lane = lax.broadcasted_iota(jnp.int32, block.shape, 1)
-    zero = jnp.zeros_like(block)
-    left = jnp.where(lane < head_dim, block, zero)
-    right = jnp.where(lane < head_dim, zero, block)
-    return jnp.concatenate([left, right], axis=0)
-
-
-def dot_t(a, b):
-    return lax.dot_general(a, b, (((1,), (1,)), ((), ())), preferred_element_type=jnp.float32)
-
-
 def own_kernel(tiles_dev, groups, tile_rows, head_dim, devices):
     scale = LOG2E / math.sqrt(head_dim)
-
-    def body(q_ref, k_ref, v_ref, g_ref, kv_ref, vkt_ref, qgt_ref, mix_ref, dot_ref, stat_ref,
-             table_ref, *pd_refs):
+    starts = offsets_of(tiles_dev, tile_rows)
+
+    def body(q_hbm, k_hbm, v_hbm, g_hbm, kv_ref, vkt_ref, qgt_ref, stat_ref, table_ref, mix_hbm,
+             pd_hbm, q_ref, k_ref, v_ref, g_ref, mix_ref, pd_ref, in_sem, out_sem):
+        loads = [
+            pltpu.make_async_copy(src, dst, in_sem.at[index])
+            for index, (src, dst) in enumerate(((k_hbm, k_ref), (v_hbm, v_ref), (q_hbm, q_ref), (g_hbm, g_ref)))
+        ]
+        for load in loads:
+            load.start()
+        for load in loads:
+            load.wait()
         sub = lax.broadcasted_iota(jnp.int32, (tile_rows, tile_rows), 0)
         lane = lax.broadcasted_iota(jnp.int32, (tile_rows, tile_rows), 1)
         causal = sub <= lane
+        stores = []
         for head in range(groups):
             cols = slice(head * head_dim, (head + 1) * head_dim)
             k_head = k_ref[:, cols]
             v_head = v_ref[:, cols]
             kv_ref[head] = jnp.concatenate([k_head, v_head], axis=1)
             vkt_ref[head] = jnp.concatenate([v_head, k_head], axis=1).T
-            qgt_ref[head] = jnp.concatenate([q_ref[:, cols], g_ref[:, cols]], axis=1).T
+            block_all = jnp.concatenate([q_ref[:, cols], g_ref[:, cols]], axis=1)
+            qgt_ref[head] = block_all.T
             for tile in range(tiles_dev):
                 rows = slice(tile * tile_rows, (tile + 1) * tile_rows)
                 span = (tile + 1) * tile_rows
                 code = tile * groups + head
-                block = jnp.concatenate([q_ref[rows, cols], g_ref[rows, cols]], axis=1)
-                both = dot_t(kv_ref[head, :span, :], paired(block, head_dim))
-                scores = both[:, :tile_rows] * scale
+                q_half, g_half = halves(block_all[rows], head_dim)
+                scores = dot_t(kv_ref[head, :span, :], q_half)
                 last = jnp.where(causal, scores[span - tile_rows :], masked_value)
+                peak = jnp.max(last, axis=0, keepdims=True)
                 if tile:
-                    scores = jnp.concatenate([scores[: span - tile_rows], last], axis=0)
-                else:
-                    scores = last
-                pair, lse, mean_grad, inverse = soft_parts(scores, both[:, tile_rows:])
+                    peak = jnp.maximum(peak, jnp.max(scores[: span - tile_rows], axis=0, keepdims=True))
+                peak = peak * scale
+                total = jnp.zeros((1, tile_rows), jnp.float32)
+                mean_grad = jnp.zeros((1, tile_rows), jnp.float32)
                 for part in range(tile + 1):
-                    pd_refs[part][head, :, (tile - part) * 2 * tile_rows : (tile - part + 1) * 2 * tile_rows] = (
-                        pair[part * tile_rows : (part + 1) * tile_rows]
-                    )
-                result = jnp.dot(vkt_ref[head, :, :span], pair, preferred_element_type=jnp.float32)
-                mix_ref[code] = result[:, :tile_rows] * inverse
-                dot_ref[code] = result[head_dim:, tile_rows:] * inverse
+                    chunk = slice(part * tile_rows, (part + 1) * tile_rows)
+                    piece = last if part == tile else scores[chunk]
+                    powers = jnp.exp2(piece * scale - peak)
+                    spread = powers * dot_t(kv_ref[head, chunk, :], g_half)
+                    total = total + jnp.sum(powers, axis=0, keepdims=True)
+                    mean_grad = mean_grad + jnp.sum(spread, axis=0, keepdims=True)
+                    at = starts[part] + (tile - part) * 2 * tile_rows
+                    pd_ref[head, :, at : at + tile_rows] = powers.astype(jnp.bfloat16)
+                    pd_ref[head, :, at + tile_rows : at + 2 * tile_rows] = spread.astype(jnp.bfloat16)
+                inverse = 1.0 / total
+                mean_grad = mean_grad * inverse
+                lse = peak + jnp.log2(total)
+                top = jnp.zeros((2 * head_dim, tile_rows), jnp.float32)
+                low = jnp.zeros((head_dim, tile_rows), jnp.float32)
+                for part in range(tile + 1):
+                    chunk = slice(part * tile_rows, (part + 1) * tile_rows)
+                    at = starts[part] + (tile - part) * 2 * tile_rows
+                    top = top + jnp.dot(vkt_ref[head, :, chunk], pd_ref[head, :, at : at + tile_rows],
+                                        preferred_element_type=jnp.float32)
+                    low = low + jnp.dot(vkt_ref[head, head_dim:, chunk], pd_ref[head, :, at + tile_rows : at + 2 * tile_rows],
+                                        preferred_element_type=jnp.float32)
+                mix_ref[head, tile, : 2 * head_dim, :] = (top * inverse).astype(jnp.bfloat16)
+                mix_ref[head, tile, 2 * head_dim :, :] = (low * inverse).astype(jnp.bfloat16)
                 stat_ref[0, code : code + 1, :] = lse
                 stat_ref[1, code : code + 1, :] = mean_grad
                 stat_ref[2, code : code + 1, :] = inverse
@@ -355,69 +379,157 @@
                 table_ref[code] = jnp.concatenate(
                     [jnp.broadcast_to(p, (devices, tile_rows)) for p in parts], axis=0
                 )
+            stores.append(pltpu.make_async_copy(pd_ref.at[head], pd_hbm.at[head], out_sem.at[0, head]))
+            stores.append(pltpu.make_async_copy(mix_ref.at[head], mix_hbm.at[head], out_sem.at[1, head]))
+            stores[-2].start()
+            stores[-1].start()
+        for store in stores:
+            store.wait()
 
     return body
+
+
+def parts_of(block, kv_head, tile_rows, head_dim, scale):
+    both = dot_t(kv_head, jnp.concatenate(halves(block, head_dim), axis=0))
+    scores = both[:, :tile_rows]
+    peak = jnp.max(scores, axis=0, keepdims=True) * scale
+    powers = jnp.exp2(scores * scale - peak)
+    spread = powers * both[:, tile_rows:]
+    return peak, powers, spread
 
 
 def serve_kernel(groups, tile_rows, head_dim, devices):
     scale = LOG2E / math.sqrt(head_dim)
 
-    def body(picks_ref, task_ref, recv_ref, kv_ref, vkt_ref, table_ref, send_ref, pd_ref, inv_ref, st_ref):
+    def body(picks_ref, task_ref, recv_hbm, kv_hbm, vkt_hbm, table_hbm, send_hbm, inv_hbm,
+             send_ref, inv_ref, st_ref, recv_ref, kv_ref, vkt_ref, table_ref, in_sem, out_sem):
         own = picks_ref[0, 0, 0]
+        loads = [
+            pltpu.make_async_copy(src, dst, in_sem.at[index])
+            for index, (src, dst) in enumerate(
+                ((recv_hbm, recv_ref), (kv_hbm, kv_ref), (vkt_hbm, vkt_ref), (table_hbm, table_ref))
+            )
+        ]
+        for load in loads:
+            load.start()
         st_ref[...] = jnp.zeros_like(st_ref)
         inv_ref[...] = jnp.zeros_like(inv_ref)
-
-        def turn(source, carry):
+        for load in loads:
+            load.wait()
+        heads = [None]
+        blocks = [None]
+        for source in range(1, devices):
             code = jnp.max(recv_ref[source, tile_rows:, :].astype(jnp.float32)[0:1, :]).astype(jnp.int32) - 1
-
-            @pl.when(code >= 0)
-            def _():
-                head = lax.rem(code, groups)
-                block = recv_ref[source, :tile_rows, :]
-                both = dot_t(kv_ref[head], paired(block, head_dim))
-                pair, lse, mean_grad, inverse = soft_parts(both[:, :tile_rows] * scale, both[:, tile_rows:])
-                pd_ref[source] = pair
-                result = jnp.dot(vkt_ref[head], pair, preferred_element_type=jnp.float32)
-                send_ref[source, : 2 * head_dim, :] = (result[:, :tile_rows] * inverse).astype(jnp.bfloat16)
-                send_ref[source, 2 * head_dim : 3 * head_dim, :] = (
-                    result[head_dim:, tile_rows:] * inverse
-                ).astype(jnp.bfloat16)
-                parts = split_low(lse) + split_low(mean_grad)
-                for index in range(4):
-                    st_ref[pl.ds(index * devices + source, 1), :] = parts[index]
-                inv_ref[pl.ds(source, 1), :] = inverse
-
-            return carry
-
-        lax.fori_loop(own + 1, devices, turn, 0)
+            block = recv_ref[source, :tile_rows, :]
+            heads.append(lax.rem(jnp.maximum(code, 0), groups))
+            blocks.append(jnp.where((code >= 0) & (own != source), block, jnp.zeros_like(block)))
+        ahead = parts_of(blocks[1], kv_ref[heads[1]], tile_rows, head_dim, scale)
+        for source in range(1, devices):
+            peak, powers, spread = ahead
+            if source + 1 < devices:
+                ahead = parts_of(blocks[source + 1], kv_ref[heads[source + 1]], tile_rows, head_dim, scale)
+            total = jnp.sum(powers, axis=0, keepdims=True)
+            inverse = 1.0 / total
+            mean_grad = jnp.sum(spread, axis=0, keepdims=True) * inverse
+            both = jnp.concatenate([powers.astype(jnp.bfloat16), spread.astype(jnp.bfloat16)], axis=1)
+            result = jnp.dot(vkt_ref[heads[source]], both, preferred_element_type=jnp.float32)
+            send_ref[source, : 2 * head_dim, :] = (result[:, :tile_rows] * inverse).astype(jnp.bfloat16)
+            send_ref[source, 2 * head_dim : 3 * head_dim, :] = (result[head_dim:, tile_rows:] * inverse).astype(jnp.bfloat16)
+            parts = split_low(peak + jnp.log2(total)) + split_low(mean_grad)
+            for index in range(4):
+                st_ref[index * devices + source : index * devices + source + 1, :] = parts[index]
+            inv_ref[source : source + 1, :] = inverse
         table = st_ref[...]
         row = lax.broadcasted_iota(jnp.int32, table.shape, 0)
         mine = lax.rem(row, devices) == own
         for peer in range(devices):
             code = jnp.maximum(task_ref[peer], 0)
             send_ref[peer, 3 * head_dim :, :] = jnp.where(mine, table_ref[code], table).astype(jnp.bfloat16)
+        stores = [
+            pltpu.make_async_copy(send_ref, send_hbm, out_sem.at[0]),
+            pltpu.make_async_copy(inv_ref, inv_hbm, out_sem.at[1]),
+        ]
+        for store in stores:
+            store.start()
+        for store in stores:
+            store.wait()
 
     return body
 
 
-def flip_kernel(devices, tile_rows):
-    def body(recv_ref, qgt_ref):
-        for source in range(1, devices):
-            qgt_ref[source] = recv_ref[source, :tile_rows, :].T
+def again_kernel(groups, tile_rows, head_dim, devices):
+    scale = LOG2E / math.sqrt(head_dim)
+
+    def body(picks_ref, recv_ref, kv_ref, pd_ref, qgt_ref):
+        own = picks_ref[0, 0, 0]
+
+        def turn(source, carry):
+            code = jnp.max(recv_ref[source, tile_rows:, :].astype(jnp.float32)[0:1, :]).astype(jnp.int32) - 1
+            block = recv_ref[source, :tile_rows, :]
+            block = jnp.where((code >= 0) & (own != source), block, jnp.zeros_like(block))
+            head = lax.rem(jnp.maximum(code, 0), groups)
+            _, powers, spread = parts_of(block, kv_ref[head], tile_rows, head_dim, scale)
+            pd_ref[source, :, :tile_rows] = powers.astype(jnp.bfloat16)
+            pd_ref[source, :, tile_rows:] = spread.astype(jnp.bfloat16)
+            qgt_ref[source] = block.T
+            return carry
+
+        lax.fori_loop(1, devices, turn, 0)
 
     return body
 
 
 def final_kernel(tiles_dev, groups, picked, tile_rows, head_dim, devices):
     scaling = 1.0 / math.sqrt(head_dim)
-
-    def body(picks_ref, task_ref, recv_ref, back_ref, qgt_ref, qgt_in_ref, mix_ref, dot_ref, stat_ref,
-             inv_ref, pd_in_ref, *rest):
-        pd_refs = rest[:tiles_dev]
-        out_ref, dq_ref, dk_ref, dv_ref, acc_ref, grad_ref, lse_sc, gd_sc, w_sc, d_sc, x_ref = rest[tiles_dev:]
+    starts = offsets_of(tiles_dev, tile_rows)
+    pair = 2 * tile_rows
+
+    def body(picks_ref, task_ref, recv_hbm, back_hbm, qgt_hbm, qgt_in_hbm, stat_hbm, inv_hbm,
+             mix_hbm, pd_in_hbm, pd_hbm, out_hbm, dq_hbm, dk_hbm, dv_hbm,
+             meta_ref, back_ref, qgt_ref, qgt_in_ref, stat_ref, inv_ref,
+             mix_ref, pd_in_ref, pd_ref, out_ref, dq_ref, dk_ref, dv_ref, acc_ref, grad_ref, more_ref,
+             lse_sc, gd_sc, w_sc, d_sc, x_ref, xin_ref, load_sem, pd_sem, in_sem, out_sem):
         own = picks_ref[0, 0, 0]
         tasks = tiles_dev * groups
         base = 3 * head_dim
+        loads = [
+            pltpu.make_async_copy(src, dst, load_sem.at[index])
+            for index, (src, dst) in enumerate(
+                (
+                    (back_hbm, back_ref),
+                    (recv_hbm.at[:, tile_rows : tile_rows + 16, :], meta_ref),
+                    (stat_hbm, stat_ref),
+                    (inv_hbm, inv_ref),
+                    (mix_hbm, mix_ref),
+                    (qgt_hbm, qgt_ref),
+                    (qgt_in_hbm, qgt_in_ref),
+                )
+            )
+        ]
+        owns = [
+            [
+                pltpu.make_async_copy(
+                    pd_hbm.at[head, :, starts[part] : starts[part + 1]],
+                    pd_ref.at[head, part * tile_rows : (part + 1) * tile_rows, part * pair :],
+                    pd_sem.at[head, part],
+                )
+                for part in range(tiles_dev)
+            ]
+            for head in range(groups)
+        ]
+        ins = [None] + [
+            pltpu.make_async_copy(pd_in_hbm.at[s], pd_in_ref.at[s], in_sem.at[s]) for s in range(1, devices)
+        ]
+        for copy in loads + [copy for row in owns for copy in row] + ins[1:]:
+            copy.start()
+        more_ref[...] = jnp.zeros_like(more_ref)
+        for head in range(groups):
+            for part in range(1, tiles_dev, 2):
+                pd_ref[head, part * tile_rows : (part + 1) * tile_rows, (part - 1) * pair : part * pair] = jnp.zeros(
+                    (tile_rows, pair), jnp.bfloat16
+                )
+        for load in loads[:4]:
+            load.wait()
 
         lse_of = []
         gd_of = []
@@ -429,15 +541,17 @@
             gd_sc[peer] = gd_of[peer]
 
         ids = lax.broadcasted_iota(jnp.int32, (devices, tile_rows), 0)
-        metas = [recv_ref[source, tile_rows : tile_rows + 16, :].astype(jnp.float32) for source in range(devices)]
-        lists = [
+        metas = [meta_ref[source].astype(jnp.float32) for source in range(devices)]
+        rows_of = [
             jnp.concatenate([metas[source][entry : entry + 1] for source in range(devices)], axis=0).astype(jnp.int32)
-            for entry in range(1, picked)
+            for entry in range(picked)
         ]
+        codes = [None] + [jnp.max(metas[source][0:1, :]).astype(jnp.int32) - 1 for source in range(1, devices)]
+        live = (rows_of[0] > 0) & (ids != own)
         chosen = []
         for peer in range(devices):
             active = ids == peer
-            for entry in lists:
+            for entry in rows_of[1:]:
                 active = active | (entry == peer)
             chosen.append(active)
         peak = jnp.full((devices, tile_rows), masked_value, jnp.float32)
@@ -450,10 +564,9 @@
             total = total + power
             delta = delta + jnp.where(chosen[peer], power * gd_of[peer], 0.0)
         delta = delta / total
-        mine_gd = gd_sc[own]
         weight = jnp.exp2(lse_sc[own] - peak) / total * inv_ref[...]
-        w_sc[0] = weight
-        w_sc[1] = weight * (mine_gd - delta)
+        w_sc[0] = jnp.where(live, weight, 0.0)
+        w_sc[1] = jnp.where(live, -weight * delta, 0.0)
 
         code_ids = lax.broadcasted_iota(jnp.int32, (tasks, tile_rows), 0)
         own_lse = stat_ref[0]
@@ -479,15 +592,18 @@
         d_sc[2] = delta
         d_sc[3] = own_weight
         d_sc[4] = own_weight * stat_ref[2]
-        d_sc[5] = own_weight * stat_ref[2] * (own_gd - delta)
-        d_sc[6] = own_weight * (own_gd - delta)
-
-        for code in range(tasks):
-            mix = mix_ref[code]
-            acc_ref[code, :head_dim, :] = mix[:head_dim] * d_sc[3, code : code + 1, :]
-            acc_ref[code, head_dim:, :] = (
-                dot_ref[code] * d_sc[3, code : code + 1, :] + mix[head_dim:] * d_sc[6, code : code + 1, :]
-            )
+        d_sc[5] = -own_weight * stat_ref[2] * delta
+        d_sc[6] = -own_weight * delta
+
+        loads[4].wait()
+        for head in range(groups):
+            for tile in range(tiles_dev):
+                code = tile * groups + head
+                first = d_sc[3, code : code + 1, :]
+                second = d_sc[6, code : code + 1, :]
+                mix = mix_ref[head, tile].astype(jnp.float32)
+                acc_ref[0, code] = mix[:head_dim] * first
+                acc_ref[1, code] = mix[2 * head_dim :] * first + mix[head_dim : 2 * head_dim] * second
 
         def gather(peer, carry):
             code = task_ref[peer]
@@ -496,59 +612,85 @@
             def _():
                 at = pl.ds(code, 1)
                 part_w = jnp.exp2(lse_sc[peer, pl.ds(own, 1), :] - d_sc[0, at, :]) * d_sc[1, at, :]
-                shift = part_w * (gd_sc[peer, pl.ds(own, 1), :] - d_sc[2, at, :])
-                mix = back_ref[peer, : 2 * head_dim, :].astype(jnp.float32)
-                low = back_ref[peer, 2 * head_dim : 3 * head_dim, :].astype(jnp.float32)
-                acc_ref[code, :head_dim, :] += mix[:head_dim] * part_w
-                acc_ref[code, head_dim:, :] += low * part_w + mix[head_dim:] * shift
+                shift = -part_w * d_sc[2, at, :]
+                mix = back_ref[peer, : 3 * head_dim, :].astype(jnp.float32)
+                acc_ref[0, code] += mix[:head_dim] * part_w
+                acc_ref[1, code] += mix[2 * head_dim :] * part_w + mix[head_dim : 2 * head_dim] * shift
 
             return carry
 
         lax.fori_loop(0, own, gather, 0)
 
+        sub = lax.broadcasted_iota(jnp.int32, (tile_rows, tile_rows), 0)
+        lane = lax.broadcasted_iota(jnp.int32, (tile_rows, tile_rows), 1)
+        unit = jnp.where(sub == lane, 1.0, 0.0).astype(jnp.bfloat16)
+        for tile in range(tiles_dev):
+            rows = slice(tile * tile_rows, (tile + 1) * tile_rows)
+            for head in range(0, groups, 2):
+                cols = slice(head * head_dim, (head + 2) * head_dim)
+                code = tile * groups + head
+                both = jnp.concatenate([acc_ref[0, code], acc_ref[0, code + 1]], axis=0).astype(jnp.bfloat16)
+                out_ref[rows, cols] = dot_t(unit, both).astype(jnp.bfloat16)
+                both = jnp.concatenate([acc_ref[1, code], acc_ref[1, code + 1]], axis=0)
+                dq_ref[rows, cols] = dot_t(unit, (both * scaling).astype(jnp.bfloat16)).astype(jnp.bfloat16)
+        stores = [
+            pltpu.make_async_copy(src, dst, out_sem.at[index])
+            for index, (src, dst) in enumerate(((out_ref, out_hbm), (dq_ref, dq_hbm), (dk_ref, dk_hbm), (dv_ref, dv_hbm)))
+        ]
+        stores[0].start()
+        stores[1].start()
+
+        for copy in loads[5:] + [copy for row in owns for copy in row] + ins[1:]:
+            copy.wait()
+        nothing = jnp.zeros((head_dim, tile_rows), jnp.bfloat16)
         for head in range(groups):
+            v_rows = slice(0, head_dim) if head % 2 == 0 else slice(head_dim, 2 * head_dim)
+            k_rows = slice(head_dim, 2 * head_dim) if head % 2 == 0 else slice(0, head_dim)
             for tile in range(tiles_dev):
                 code = tile * groups + head
                 first = d_sc[4, code : code + 1, :]
                 second = d_sc[5, code : code + 1, :]
                 turned = qgt_ref[head, :, tile * tile_rows : (tile + 1) * tile_rows].astype(jnp.float32)
-                at = tile * 2 * tile_rows
-                x_ref[:head_dim, at : at + tile_rows] = (turned[head_dim:] * first).astype(jnp.bfloat16)
-                x_ref[:head_dim, at + tile_rows : at + 2 * tile_rows] = jnp.zeros((head_dim, tile_rows), jnp.bfloat16)
-                x_ref[head_dim:, at : at + tile_rows] = (turned[:head_dim] * second).astype(jnp.bfloat16)
-                x_ref[head_dim:, at + tile_rows : at + 2 * tile_rows] = (turned[:head_dim] * first).astype(jnp.bfloat16)
+                early = slice(tile * pair, tile * pair + tile_rows)
+                late = slice(tile * pair + tile_rows, (tile + 1) * pair)
+                x_ref[head, v_rows, early] = (turned[head_dim:] * first).astype(jnp.bfloat16)
+                x_ref[head, v_rows, late] = nothing
+                x_ref[head, k_rows, early] = (turned[:head_dim] * second).astype(jnp.bfloat16)
+                x_ref[head, k_rows, late] = (turned[:head_dim] * first).astype(jnp.bfloat16)
+        for source in range(1, devices):
+            odd = lax.rem(jnp.maximum(codes[source], 0), 2) == 1
+            first = w_sc[0, source : source + 1, :]
+            second = w_sc[1, source : source + 1, :]
+            turned = qgt_in_ref[source].astype(jnp.float32)
+            g_first = (turned[head_dim:] * first).astype(jnp.bfloat16)
+            q_first = (turned[:head_dim] * first).astype(jnp.bfloat16)
+            q_second = (turned[:head_dim] * second).astype(jnp.bfloat16)
+            xin_ref[source, :head_dim, :tile_rows] = jnp.where(odd, q_second, g_first)
+            xin_ref[source, :head_dim, tile_rows:] = jnp.where(odd, q_first, nothing)
+            xin_ref[source, head_dim:, :tile_rows] = jnp.where(odd, g_first, q_second)
+            xin_ref[source, head_dim:, tile_rows:] = jnp.where(odd, nothing, q_first)
+        for head in range(groups):
+            for first in range(0, tiles_dev, 2):
+                rows = slice(first * tile_rows, (first + 2) * tile_rows)
+                grad_ref[head, rows, :] = dot_t(pd_ref[head, rows, first * pair :], x_ref[head, :, first * pair :])
+        for source in range(1, devices):
+            head = lax.rem(jnp.maximum(codes[source], 0), groups)
+            target = grad_ref if source % 2 else more_ref
+            target[head] += dot_t(pd_in_ref[source], xin_ref[source])
+        lane = lax.broadcasted_iota(jnp.int32, (tile_rows, 2 * head_dim), 1)
+        for head in range(0, groups, 2):
+            cols = slice(head * head_dim, (head + 2) * head_dim)
             for part in range(tiles_dev):
-                grad_ref[head, part * tile_rows : (part + 1) * tile_rows, :] = dot_t(
-                    pd_refs[part][head], x_ref[:, part * 2 * tile_rows :]
-                )
-
-        def spread(source, carry):
-            code = jnp.max(recv_ref[source, tile_rows:, :].astype(jnp.float32)[0:1, :]).astype(jnp.int32) - 1
-
-            @pl.when(code >= 0)
-            def _():
-                head = lax.rem(code, groups)
-                first = w_sc[0, pl.ds(source, 1), :]
-                second = w_sc[1, pl.ds(source, 1), :]
-                turned = qgt_in_ref[source].astype(jnp.float32)
-                top = jnp.concatenate([turned[head_dim:] * first, jnp.zeros((head_dim, tile_rows), jnp.float32)], axis=1)
-                low = jnp.concatenate([turned[:head_dim] * second, turned[:head_dim] * first], axis=1)
-                factor = jnp.concatenate([top, low], axis=0).astype(jnp.bfloat16)
-                grad_ref[head] += dot_t(pd_in_ref[source], factor)
-
-            return carry
-
-        lax.fori_loop(own + 1, devices, spread, 0)
-
-        for head in range(groups):
-            cols = slice(head * head_dim, (head + 1) * head_dim)
-            dv_ref[:, cols] = grad_ref[head, :, :head_dim].astype(jnp.bfloat16)
-            dk_ref[:, cols] = (grad_ref[head, :, head_dim:] * scaling).astype(jnp.bfloat16)
-            for tile in range(tiles_dev):
-                rows = slice(tile * tile_rows, (tile + 1) * tile_rows)
-                turned = acc_ref[tile * groups + head].T
-                out_ref[rows, cols] = turned[:, :head_dim].astype(jnp.bfloat16)
-                dq_ref[rows, cols] = (turned[:, head_dim:] * scaling).astype(jnp.bfloat16)
+                rows = slice(part * tile_rows, (part + 1) * tile_rows)
+                even = grad_ref[head, rows, :] + more_ref[head, rows, :]
+                odd = grad_ref[head + 1, rows, :] + more_ref[head + 1, rows, :]
+                dv_ref[rows, cols] = jnp.where(lane < head_dim, even, odd).astype(jnp.bfloat16)
+                swapped = jnp.where(lane < head_dim, odd, even) * scaling
+                dk_ref[rows, cols] = pltpu.roll(swapped, head_dim, 1).astype(jnp.bfloat16)
+        stores[2].start()
+        stores[3].start()
+        for store in stores:
+            store.wait()
 
     return body
 
@@ -562,10 +704,15 @@
     tasks = tiles_dev * groups
     smem = pl.BlockSpec(memory_space=pltpu.SMEM)
     vmem = pl.BlockSpec(memory_space=pltpu.VMEM)
+    far = pl.BlockSpec(memory_space=pltpu.HBM)
     low = jnp.bfloat16
     wide = jnp.float32
     width = 2 * head_dim
     shape = jax.ShapeDtypeStruct
+    dma = pltpu.SemaphoreType.DMA
+    small = pltpu.CompilerParams(vmem_limit_bytes=vmem_grant)
+    large = pltpu.CompilerParams(vmem_limit_bytes=vmem_whole)
+    pair_cols = offsets_of(tiles_dev, tile_rows)[-1]
 
     send_q, task_of = pl.pallas_call(
         pack_kernel(tiles_dev, groups, picked, tile_rows, head_dim, devices),
@@ -576,64 +723,95 @@
     )(picks, query, grad_out)
     recv_q = lax.all_to_all(send_q, "ctx", split_axis=0, concat_axis=0, tiled=True)
 
-    own_shapes = (
-        shape((groups, row_count, width), low),
-        shape((groups, width, row_count), low),
-        shape((groups, width, row_count), low),
-        shape((tasks, width, tile_rows), wide),
-        shape((tasks, head_dim, tile_rows), wide),
-        shape((3, tasks, tile_rows), wide),
-        shape((tasks, 4 * devices, tile_rows), wide),
-    ) + tuple(
-        shape((groups, tile_rows, (tiles_dev - part) * 2 * tile_rows), low) for part in range(tiles_dev)
-    )
-    kv, vkt, qgt, mix, dots, stats, table, *pairs = pl.pallas_call(
+    mix_shape = (groups, tiles_dev, 3 * head_dim, tile_rows)
+    pair_shape = (groups, tile_rows, pair_cols)
+    kv, vkt, qgt, stats, table, mix, pairs = pl.pallas_call(
         own_kernel(tiles_dev, groups, tile_rows, head_dim, devices),
-        out_shape=own_shapes,
-        in_specs=[vmem] * 4,
-        out_specs=tuple([vmem] * len(own_shapes)),
+        out_shape=(
+            shape((groups, row_count, width), low),
+            shape((groups, width, row_count), low),
+            shape((groups, width, row_count), low),
+            shape((3, tasks, tile_rows), wide),
+            shape((tasks, 4 * devices, tile_rows), wide),
+            shape(mix_shape, low),
+            shape(pair_shape, low),
+        ),
+        in_specs=[far] * 4,
+        out_specs=(vmem, vmem, vmem, vmem, vmem, far, far),
+        scratch_shapes=[pltpu.VMEM((row_count, columns), low)] * 4
+        + [pltpu.VMEM(mix_shape, low), pltpu.VMEM(pair_shape, low), dma((4,)), dma((2, groups))],
+        compiler_params=large,
         name="own",
     )(query, key, value, grad_out)
 
     slot = 3 * head_dim + 4 * devices
-    send_b, pairs_in, inverse_in = pl.pallas_call(
+    in_shape = (devices, row_count, 2 * tile_rows)
+    send_b, inverse_in = pl.pallas_call(
         serve_kernel(groups, tile_rows, head_dim, devices),
-        out_shape=(
-            shape((devices, slot, tile_rows), low),
-            shape((devices, row_count, 2 * tile_rows), low),
-            shape((devices, tile_rows), wide),
-        ),
-        in_specs=[smem, smem, vmem, vmem, vmem, vmem],
-        out_specs=(vmem, vmem, vmem),
-        scratch_shapes=[pltpu.VMEM((4 * devices, tile_rows), wide)],
+        out_shape=(shape((devices, slot, tile_rows), low), shape((devices, tile_rows), wide)),
+        in_specs=[smem, smem, far, far, far, far],
+        out_specs=(far, far),
+        scratch_shapes=[
+            pltpu.VMEM((devices, slot, tile_rows), low),
+            pltpu.VMEM((devices, tile_rows), wide),
+            pltpu.VMEM((4 * devices, tile_rows), wide),
+            pltpu.VMEM(send_q.shape, low),
+            pltpu.VMEM(kv.shape, low),
+            pltpu.VMEM(vkt.shape, low),
+            pltpu.VMEM(table.shape, wide),
+            dma((4,)),
+            dma((2,)),
+        ],
+        compiler_params=small,
         name="serve",
     )(picks, task_of, recv_q, kv, vkt, table)
     recv_b = lax.all_to_all(send_b, "ctx", split_axis=0, concat_axis=0, tiled=True)
 
-    qgt_in = pl.pallas_call(
-        flip_kernel(devices, tile_rows),
-        out_shape=shape((devices, width, tile_rows), low),
-        in_specs=[vmem],
-        out_specs=vmem,
-        name="flip",
-    )(recv_q)
-
+    pairs_in, qgt_in = pl.pallas_call(
+        again_kernel(groups, tile_rows, head_dim, devices),
+        out_shape=(shape(in_shape, low), shape((devices, width, tile_rows), low)),
+        in_specs=[smem, vmem, vmem],
+        out_specs=(vmem, vmem),
+        compiler_params=large,
+        name="again",
+    )(picks, recv_q, kv)
+
+    square = (groups, row_count, 2 * row_count)
     return pl.pallas_call(
         final_kernel(tiles_dev, groups, picked, tile_rows, head_dim, devices),
         out_shape=tuple([shape((row_count, columns), low)] * 4),
-        in_specs=[smem, smem] + [vmem] * (9 + tiles_dev),
-        out_specs=tuple([vmem] * 4),
+        in_specs=[smem, smem] + [far] * 9,
+        out_specs=tuple([far] * 4),
         scratch_shapes=[
-            pltpu.VMEM((tasks, width, tile_rows), wide),
+            pltpu.VMEM((devices, 16, width), low),
+            pltpu.VMEM((devices, slot, tile_rows), low),
+            pltpu.VMEM(qgt.shape, low),
+            pltpu.VMEM(qgt_in.shape, low),
+            pltpu.VMEM(stats.shape, wide),
+            pltpu.VMEM(inverse_in.shape, wide),
+            pltpu.VMEM(mix_shape, low),
+            pltpu.VMEM(in_shape, low),
+            pltpu.VMEM(square, low),
+        ]
+        + [pltpu.VMEM((row_count, columns), low)] * 4
+        + [
+            pltpu.VMEM((2, tasks, head_dim, tile_rows), wide),
+            pltpu.VMEM((groups, row_count, width), wide),
             pltpu.VMEM((groups, row_count, width), wide),
             pltpu.VMEM((devices, devices, tile_rows), wide),
             pltpu.VMEM((devices, devices, tile_rows), wide),
             pltpu.VMEM((2, devices, tile_rows), wide),
             pltpu.VMEM((7, tasks, tile_rows), wide),
-            pltpu.VMEM((width, 2 * row_count), low),
+            pltpu.VMEM((groups, width, 2 * row_count), low),
+            pltpu.VMEM((devices, width, 2 * tile_rows), low),
+            dma((7,)),
+            dma((groups, tiles_dev)),
+            dma((devices,)),
+            dma((4,)),
         ],
+        compiler_params=small,
         name="final",
-    )(picks, task_of, recv_q, recv_b, qgt, qgt_in, mix, dots, stats, inverse_in, pairs_in, *pairs)
+    )(picks, task_of, recv_q, recv_b, qgt, qgt_in, stats, inverse_in, mix, pairs_in, pairs)
 
 
 def choose(query, key, value, grad_out, picks):

time: 53.6 us -> 49 us (0.914)
  waiting for transfers between devices: 11.2 us -> 8.76 us
  Pallas kernels: 29 us -> 27.3 us
  local copies, waits for them, and re-layouts: 1.53 us -> 0 us
  starting transfers between devices: 10.8 us -> 11.8 us
    pallas_call x1, Pallas kernels: 1.8 us -> 5.43 us  [fast_local(): pl.pallas_call(again_kernel(groups, tile_rows, head_dim, devices), out_sh...]
    pallas_call x1, Pallas kernels: 8.2 us -> 4.72 us  [fast_local(): pl.pallas_call(serve_kernel(groups, tile_rows, head_dim, devices), out_sh...]
    all_to_all x1, waiting for transfers between devices: 10 us -> 7.24 us  [fast_local(): lax.all_to_all(send_b, 'ctx', split_axis=0, concat_axis=0, tiled=True)]
    pallas_call x1, Pallas kernels: 8.46 us -> 6.87 us  [fast_local(): pl.pallas_call(final_kernel(tiles_dev, groups, picked, tile_rows, head_di...]
    unnamed x4 -> x0, local copies, waits for them, and re-layouts: 1.53 us -> none
    all_to_all x1, starting transfers between devices: 3.47 us -> 4.5 us  [fast_local(): lax.all_to_all(send_b, 'ctx', split_axis=0, concat_axis=0, tiled=True)]
  transfers between devices with their start and end apart: 2 -> 2, of which waited for: 2 -> 2; matrix products, arithmetic and copies ran while one was open for 0% -> 0% of each run, Pallas kernels for 19% -> 28%
where the time goes in v2:
time: 49 us; the launch traced here: 48.5 us
  Pallas kernels  27.3 us (56%)
  starting transfers between devices  11.8 us (24%)
  waiting for transfers between devices  8.76 us (18%)
  between operations  0.66 us (1%)
    pallas_call x1, Pallas kernels, fast_local(): pl.pallas_call(own_kernel(tiles_dev, groups, tile_rows, head_dim, devices...  8.18 us
    all_to_all x1, starting transfers between devices, fast_local(): lax.all_to_all(send_q, 'ctx', split_axis=0, concat_axis=0, tiled=True)  7.29 us
    all_to_all x1, waiting for transfers between devices, fast_local(): lax.all_to_all(send_b, 'ctx', split_axis=0, concat_axis=0, tiled=True)  7.24 us
    pallas_call x1, Pallas kernels, fast_local(): pl.pallas_call(final_kernel(tiles_dev, groups, picked, tile_rows, head_di...  6.87 us
    pallas_call x1, Pallas kernels, fast_local(): pl.pallas_call(again_kernel(groups, tile_rows, head_dim, devices), out_sh...  5.43 us
    pallas_call x1, Pallas kernels, fast_local(): pl.pallas_call(serve_kernel(groups, tile_rows, head_dim, devices), out_sh...  4.72 us
    all_to_all x1, starting transfers between devices, fast_local(): lax.all_to_all(send_b, 'ctx', split_axis=0, concat_axis=0, tiled=True)  4.5 us
    pallas_call x1, Pallas kernels, fast_local(): pl.pallas_call(pack_kernel(tiles_dev, groups, picked, tile_rows, head_dim...  2.1 us
  transfers between devices with their start and end apart: 2, of which 2 were waited for; matrix products, arithmetic and copies ran while one was open for 0% of the time, Pallas kernels for 28%

profile of v2, /device:TPU:0, one launch (start us, length us, event | category | flops | bytes accessed | tf_op | source)
XLA Modules:
  0.0 48.5 jit_solution(16461703054157147055)
XLA Ops:
  0.6 2.1 %pack.1 = (bf16[8,144,128]{2,1,0:T(8,128)(2,1)}, s32[8]{0:T(128)}) custom-call(s32[4,4,4]{2,1,0:T(4,128)} %picks_ref.7, bf16[512,256]{1,0:T(8,128)(2,1)} %q_hbm.1, bf16[512,256]{1,0:T(8,128)(2,1)} %g_hbm.1), custom_call_target="tpu_custom_call" | custom-call | tf_op jit(solution)/shard_map/pack/pallas_call | solution.py:717
  2.7 7.3 %all-to-all-start = ((bf16[8,144,128]{2,1,0:T(8,128)(2,1)}), bf16[8,144,128]{2,1,0:T(8,128)(2,1)}, u32[]{:S(2)}, u32[]{:S(2)}) async-start(bf16[8,144,128]{2,1,0:T(8,128)(2,1)} %get-tuple-element.18), calls=%async_computation | async-start | bytes 589824 | tf_op jit(solution)/shard_map/all_to_all | solution.py:724
  10.0 8.2 %own.1 = (bf16[4,512,128]{2,1,0:T(8,128)(2,1)}, bf16[4,128,512]{2,1,0:T(8,128)(2,1)}, bf16[4,128,512]{2,1,0:T(8,128)(2,1)}, f32[3,16,128]{2,1,0:T(8,128)}, f32[1...) custom-call(bf16[512,256]{1,0:T(8,128)(2,1)} %q_hbm.1, bf16[512,256]{1,0:T(8,128)(2,1)} %k_hbm.1, ...), custom_call_target="tpu_custom_call" | custom-call | tf_op jit(solution)/shard_map/own/pallas_call | solution.py:728
  18.2 1.5 %all-to-all-done.recv_hbm.recv_ref = bf16[8,144,128]{2,1,0:T(8,128)(2,1)} async-done(((bf16[8,144,128]{2,1,0:T(8,128)(2,1)}), bf16[8,144,128]{2,1,0:T(8,128)(2,1)}, u32[]{:S(2)}, u32[]{:S(2)}) %all-to-all-start) | async-done | bytes 294944 | tf_op jit(solution)/shard_map/all_to_all | solution.py:724
  19.7 4.7 %serve.1 = (bf16[8,224,128]{2,1,0:T(8,128)(2,1)}, f32[8,128]{1,0:T(8,128)}) custom-call(s32[4,4,4]{2,1,0:T(4,128)} %picks_ref.7, s32[8]{0:T(128)} %get-tuple-element.17.task_ref, bf16[8,144,128]{2,1,0:T(8,128)(2,1)} %all-to-all-done.recv_hbm.recv_ref, bf16[4,512,128]{2,1,0:T(8,128)(2,1)} %get-tuple-element.19.kv_hbm.kv_ref, ...), custom_call_target="tpu_custom_call" | custom-call | tf_op jit(solution)/shard_map/serve/pallas_call | solution.py:749
  24.5 4.5 %all-to-all-start.1 = ((bf16[8,224,128]{2,1,0:T(8,128)(2,1)}), bf16[8,224,128]{2,1,0:T(8,128)(2,1)}, u32[]{:S(2)}, u32[]{:S(2)}) async-start(bf16[8,224,128]{2,1,0:T(8,128)(2,1)} %get-tuple-element.22), calls=%async_computation.1 | async-start | bytes 917504 | tf_op jit(solution)/shard_map/all_to_all | solution.py:768
  29.0 5.4 %again.1 = (bf16[8,512,256]{2,1,0:T(8,128)(2,1)}, bf16[8,128,128]{2,1,0:T(8,128)(2,1)}) custom-call(s32[4,4,4]{2,1,0:T(4,128)} %picks_ref.7, bf16[8,144,128]{2,1,0:T(8,128)(2,1)} %all-to-all-done.recv_hbm.recv_ref, bf16[4,512,128]{2,1,0:T(8,128)(2,1)} %get-tuple-element.19.kv_hbm.kv_ref), custom_call_target="tpu_custom_call" | custom-call | tf_op jit(solution)/shard_map/again/pallas_call | solution.py:770
  34.4 7.2 %all-to-all-done.1.back_hbm = bf16[8,224,128]{2,1,0:T(8,128)(2,1)} async-done(((bf16[8,224,128]{2,1,0:T(8,128)(2,1)}), bf16[8,224,128]{2,1,0:T(8,128)(2,1)}, u32[]{:S(2)}, u32[]{:S(2)}) %all-to-all-start.1) | async-done | bytes 458784 | tf_op jit(solution)/shard_map/all_to_all | solution.py:768
  41.6 6.9 %final.1 = (bf16[512,256]{1,0:T(8,128)(2,1)}, bf16[512,256]{1,0:T(8,128)(2,1)}, bf16[512,256]{1,0:T(8,128)(2,1)}, bf16[512,256]{1,0:T(8,128)(2,1)}) custom-call(s32[4,4,4]{2,1,0:T(4,128)} %picks_ref.7, s32[8]{0:T(128)} %get-tuple-element.17.task_ref, bf16[8,144,128]{2,1,0:T(8,128)(2,1)} %all-to-all-done.recv_hbm.recv_ref, ...), custom_call_target="tpu_custom_call" | custom-call | tf_op jit(solution)/shard_map/final/pallas_call | solution.py:780
Async XLA Ops:
  2.7 17.0 %all-to-all-start = ((bf16[8,144,128]{2,1,0:T(8,128)(2,1)}), bf16[8,144,128]{2,1,0:T(8,128)(2,1)}, u32[]{:S(2)}, u32[]{:S(2)}) async-start(bf16[8,144,128]{2,1,0:T(8,128)(2,1)} %get-tuple-element.18), calls=%async_computation | async-start | bytes 589824 | tf_op jit(solution)/shard_map/all_to_all | solution.py:724
  24.5 17.2 %all-to-all-start.1 = ((bf16[8,224,128]{2,1,0:T(8,128)(2,1)}), bf16[8,224,128]{2,1,0:T(8,128)(2,1)}, u32[]{:S(2)}, u32[]{:S(2)}) async-start(bf16[8,224,128]{2,1,0:T(8,128)(2,1)} %get-tuple-element.22), calls=%async_computation.1 | async-start | bytes 917504 | tf_op jit(solution)/shard_map/all_to_all | solution.py:768

commit v3 on v2

--- a/solution.py
+++ b/solution.py
@@ -11,8 +11,7 @@
 highest = lax.Precision.HIGHEST
 LOG2E = math.log2(math.e)
 pair_budget = 8 << 20
-vmem_grant = 57 << 20
-vmem_whole = 65400 << 10
+vmem_grant = 32 << 20
 
 
 def attend_slots(q_slots, head_ids, k_heads, v_heads, scaling):
@@ -257,11 +256,11 @@
     return (attn_out, grad_query, grad_key, grad_value)
 
 
-def offsets_of(tiles_dev, tile_rows):
-    starts = [0]
+def pair_parts(near, far, tiles_dev, tile_rows):
     for part in range(tiles_dev):
-        starts.append(starts[-1] + (tiles_dev - part) * 2 * tile_rows)
-    return starts
+        rows = slice(part * tile_rows, (part + 1) * tile_rows)
+        cols = slice(part * 2 * tile_rows, tiles_dev * 2 * tile_rows)
+        yield near.at[:, rows, cols], far.at[:, rows, cols]
 
 
 def dot_t(a, b):
@@ -311,10 +310,9 @@
 
 def own_kernel(tiles_dev, groups, tile_rows, head_dim, devices):
     scale = LOG2E / math.sqrt(head_dim)
-    starts = offsets_of(tiles_dev, tile_rows)
-
-    def body(q_hbm, k_hbm, v_hbm, g_hbm, kv_ref, vkt_ref, qgt_ref, stat_ref, table_ref, mix_hbm,
-             pd_hbm, q_ref, k_ref, v_ref, g_ref, mix_ref, pd_ref, in_sem, out_sem):
+
+    def body(q_hbm, k_hbm, v_hbm, g_hbm, kv_ref, vkt_ref, stat_ref, table_ref, qgt_hbm, mix_hbm,
+             pd_hbm, q_ref, k_ref, v_ref, g_ref, qgt_ref, mix_ref, pd_ref, in_sem, out_sem):
         loads = [
             pltpu.make_async_copy(src, dst, in_sem.at[index])
             for index, (src, dst) in enumerate(((k_hbm, k_ref), (v_hbm, v_ref), (q_hbm, q_ref), (g_hbm, g_ref)))
@@ -326,7 +324,6 @@
         sub = lax.broadcasted_iota(jnp.int32, (tile_rows, tile_rows), 0)
         lane = lax.broadcasted_iota(jnp.int32, (tile_rows, tile_rows), 1)
         causal = sub <= lane
-        stores = []
         for head in range(groups):
             cols = slice(head * head_dim, (head + 1) * head_dim)
             k_head = k_ref[:, cols]
@@ -339,8 +336,9 @@
                 rows = slice(tile * tile_rows, (tile + 1) * tile_rows)
                 span = (tile + 1) * tile_rows
                 code = tile * groups + head
-                q_half, g_half = halves(block_all[rows], head_dim)
-                scores = dot_t(kv_ref[head, :span, :], q_half)
+                at = tile * 2 * tile_rows
+                both = dot_t(kv_ref[head, :span, :], jnp.concatenate(halves(block_all[rows], head_dim), axis=0))
+                scores = both[:, :tile_rows]
                 last = jnp.where(causal, scores[span - tile_rows :], masked_value)
                 peak = jnp.max(last, axis=0, keepdims=True)
                 if tile:
@@ -352,37 +350,35 @@
                     chunk = slice(part * tile_rows, (part + 1) * tile_rows)
                     piece = last if part == tile else scores[chunk]
                     powers = jnp.exp2(piece * scale - peak)
-                    spread = powers * dot_t(kv_ref[head, chunk, :], g_half)
+                    spread = powers * both[chunk, tile_rows:]
                     total = total + jnp.sum(powers, axis=0, keepdims=True)
                     mean_grad = mean_grad + jnp.sum(spread, axis=0, keepdims=True)
-                    at = starts[part] + (tile - part) * 2 * tile_rows
-                    pd_ref[head, :, at : at + tile_rows] = powers.astype(jnp.bfloat16)
-                    pd_ref[head, :, at + tile_rows : at + 2 * tile_rows] = spread.astype(jnp.bfloat16)
+                    pd_ref[head, chunk, at : at + tile_rows] = powers.astype(jnp.bfloat16)
+                    pd_ref[head, chunk, at + tile_rows : at + 2 * tile_rows] = spread.astype(jnp.bfloat16)
                 inverse = 1.0 / total
                 mean_grad = mean_grad * inverse
                 lse = peak + jnp.log2(total)
-                top = jnp.zeros((2 * head_dim, tile_rows), jnp.float32)
-                low = jnp.zeros((head_dim, tile_rows), jnp.float32)
-                for part in range(tile + 1):
-                    chunk = slice(part * tile_rows, (part + 1) * tile_rows)
-                    at = starts[part] + (tile - part) * 2 * tile_rows
-                    top = top + jnp.dot(vkt_ref[head, :, chunk], pd_ref[head, :, at : at + tile_rows],
-                                        preferred_element_type=jnp.float32)
-                    low = low + jnp.dot(vkt_ref[head, head_dim:, chunk], pd_ref[head, :, at + tile_rows : at + 2 * tile_rows],
-                                        preferred_element_type=jnp.float32)
+                result = jnp.dot(vkt_ref[head, :, :span], pd_ref[head, :span, at : at + 2 * tile_rows],
+                                 preferred_element_type=jnp.float32)
+                top = result[:, :tile_rows]
+                low = result[head_dim:, tile_rows:]
                 mix_ref[head, tile, : 2 * head_dim, :] = (top * inverse).astype(jnp.bfloat16)
                 mix_ref[head, tile, 2 * head_dim :, :] = (low * inverse).astype(jnp.bfloat16)
                 stat_ref[0, code : code + 1, :] = lse
                 stat_ref[1, code : code + 1, :] = mean_grad
                 stat_ref[2, code : code + 1, :] = inverse
-                parts = split_low(lse) + split_low(mean_grad)
-                table_ref[code] = jnp.concatenate(
-                    [jnp.broadcast_to(p, (devices, tile_rows)) for p in parts], axis=0
-                )
-            stores.append(pltpu.make_async_copy(pd_ref.at[head], pd_hbm.at[head], out_sem.at[0, head]))
-            stores.append(pltpu.make_async_copy(mix_ref.at[head], mix_hbm.at[head], out_sem.at[1, head]))
-            stores[-2].start()
-            stores[-1].start()
+                parts = split_low(lse) + (mean_grad,)
+                for index in range(3):
+                    table_ref[code, index : index + 1, :] = parts[index]
+        stores = [
+            pltpu.make_async_copy(mix_ref, mix_hbm, out_sem.at[tiles_dev]),
+            pltpu.make_async_copy(qgt_ref, qgt_hbm, out_sem.at[tiles_dev + 1]),
+        ] + [
+            pltpu.make_async_copy(src, dst, out_sem.at[index])
+            for index, (src, dst) in enumerate(pair_parts(pd_ref, pd_hbm, tiles_dev, tile_rows))
+        ]
+        for store in stores:
+            store.start()
         for store in stores:
             store.wait()
 
@@ -401,21 +397,11 @@
 def serve_kernel(groups, tile_rows, head_dim, devices):
     scale = LOG2E / math.sqrt(head_dim)
 
-    def body(picks_ref, task_ref, recv_hbm, kv_hbm, vkt_hbm, table_hbm, send_hbm, inv_hbm,
-             send_ref, inv_ref, st_ref, recv_ref, kv_ref, vkt_ref, table_ref, in_sem, out_sem):
+    def body(picks_ref, task_ref, recv_ref, kv_ref, vkt_ref, table_ref, send_hbm, inv_ref,
+             send_ref, st_ref, out_sem):
         own = picks_ref[0, 0, 0]
-        loads = [
-            pltpu.make_async_copy(src, dst, in_sem.at[index])
-            for index, (src, dst) in enumerate(
-                ((recv_hbm, recv_ref), (kv_hbm, kv_ref), (vkt_hbm, vkt_ref), (table_hbm, table_ref))
-            )
-        ]
-        for load in loads:
-            load.start()
         st_ref[...] = jnp.zeros_like(st_ref)
         inv_ref[...] = jnp.zeros_like(inv_ref)
-        for load in loads:
-            load.wait()
         heads = [None]
         blocks = [None]
         for source in range(1, devices):
@@ -435,8 +421,8 @@
             result = jnp.dot(vkt_ref[heads[source]], both, preferred_element_type=jnp.float32)
             send_ref[source, : 2 * head_dim, :] = (result[:, :tile_rows] * inverse).astype(jnp.bfloat16)
             send_ref[source, 2 * head_dim : 3 * head_dim, :] = (result[head_dim:, tile_rows:] * inverse).astype(jnp.bfloat16)
-            parts = split_low(peak + jnp.log2(total)) + split_low(mean_grad)
-            for index in range(4):
+            parts = split_low(peak + jnp.log2(total)) + (mean_grad,)
+            for index in range(3):
                 st_ref[index * devices + source : index * devices + source + 1, :] = parts[index]
             inv_ref[source : source + 1, :] = inverse
         table = st_ref[...]
@@ -444,15 +430,14 @@
         mine = lax.rem(row, devices) == own
         for peer in range(devices):
             code = jnp.maximum(task_ref[peer], 0)
-            send_ref[peer, 3 * head_dim :, :] = jnp.where(mine, table_ref[code], table).astype(jnp.bfloat16)
-        stores = [
-            pltpu.make_async_copy(send_ref, send_hbm, out_sem.at[0]),
-            pltpu.make_async_copy(inv_ref, inv_hbm, out_sem.at[1]),
-        ]
-        for store in stores:
-            store.start()
-        for store in stores:
-            store.wait()
+            entry = table_ref[code]
+            wide = jnp.concatenate(
+                [jnp.broadcast_to(entry[index : index + 1], (devices, tile_rows)) for index in range(3)], axis=0
+            )
+            send_ref[peer, 3 * head_dim :, :] = jnp.where(mine, wide, table).astype(jnp.bfloat16)
+        store = pltpu.make_async_copy(send_ref, send_hbm, out_sem)
+        store.start()
+        store.wait()
 
     return body
 
@@ -460,8 +445,10 @@
 def again_kernel(groups, tile_rows, head_dim, devices):
     scale = LOG2E / math.sqrt(head_dim)
 
-    def body(picks_ref, recv_ref, kv_ref, pd_ref, qgt_ref):
+    def body(picks_ref, recv_ref, kv_ref, pd_ref, qgt_ref, meta_ref):
         own = picks_ref[0, 0, 0]
+        for source in range(devices):
+            meta_ref[source] = recv_ref[source, tile_rows:, :].astype(jnp.float32)
 
         def turn(source, carry):
             code = jnp.max(recv_ref[source, tile_rows:, :].astype(jnp.float32)[0:1, :]).astype(jnp.int32) - 1
@@ -469,9 +456,9 @@
             block = jnp.where((code >= 0) & (own != source), block, jnp.zeros_like(block))
             head = lax.rem(jnp.maximum(code, 0), groups)
             _, powers, spread = parts_of(block, kv_ref[head], tile_rows, head_dim, scale)
-            pd_ref[source, :, :tile_rows] = powers.astype(jnp.bfloat16)
-            pd_ref[source, :, tile_rows:] = spread.astype(jnp.bfloat16)
-            qgt_ref[source] = block.T
+            pd_ref[source - 1, :, :tile_rows] = powers.astype(jnp.bfloat16)
+            pd_ref[source - 1, :, tile_rows:] = spread.astype(jnp.bfloat16)
+            qgt_ref[source - 1] = block.T
             return carry
 
         lax.fori_loop(1, devices, turn, 0)
@@ -481,67 +468,41 @@
 
 def final_kernel(tiles_dev, groups, picked, tile_rows, head_dim, devices):
     scaling = 1.0 / math.sqrt(head_dim)
-    starts = offsets_of(tiles_dev, tile_rows)
     pair = 2 * tile_rows
 
-    def body(picks_ref, task_ref, recv_hbm, back_hbm, qgt_hbm, qgt_in_hbm, stat_hbm, inv_hbm,
-             mix_hbm, pd_in_hbm, pd_hbm, out_hbm, dq_hbm, dk_hbm, dv_hbm,
-             meta_ref, back_ref, qgt_ref, qgt_in_ref, stat_ref, inv_ref,
-             mix_ref, pd_in_ref, pd_ref, out_ref, dq_ref, dk_ref, dv_ref, acc_ref, grad_ref, more_ref,
-             lse_sc, gd_sc, w_sc, d_sc, x_ref, xin_ref, load_sem, pd_sem, in_sem, out_sem):
+    def body(picks_ref, task_ref, meta_ref, back_ref, qgt_in_ref, stat_ref, inv_ref,
+             pd_in_ref, qgt_hbm, mix_hbm, pd_hbm, out_hbm, dq_hbm, dk_hbm, dv_hbm,
+             qgt_ref, mix_ref, pd_ref, out_ref, dq_ref, dk_ref, dv_ref, acc_ref, grad_ref, more_ref,
+             lse_sc, gd_sc, w_sc, d_sc, x_ref, xin_ref, in_sem, out_sem):
         own = picks_ref[0, 0, 0]
         tasks = tiles_dev * groups
         base = 3 * head_dim
         loads = [
-            pltpu.make_async_copy(src, dst, load_sem.at[index])
-            for index, (src, dst) in enumerate(
-                (
-                    (back_hbm, back_ref),
-                    (recv_hbm.at[:, tile_rows : tile_rows + 16, :], meta_ref),
-                    (stat_hbm, stat_ref),
-                    (inv_hbm, inv_ref),
-                    (mix_hbm, mix_ref),
-                    (qgt_hbm, qgt_ref),
-                    (qgt_in_hbm, qgt_in_ref),
-                )
-            )
+            pltpu.make_async_copy(mix_hbm, mix_ref, in_sem.at[tiles_dev]),
+            pltpu.make_async_copy(qgt_hbm, qgt_ref, in_sem.at[tiles_dev + 1]),
+        ] + [
+            pltpu.make_async_copy(src, dst, in_sem.at[index])
+            for index, (dst, src) in enumerate(pair_parts(pd_ref, pd_hbm, tiles_dev, tile_rows))
         ]
-        owns = [
-            [
-                pltpu.make_async_copy(
-                    pd_hbm.at[head, :, starts[part] : starts[part + 1]],
-                    pd_ref.at[head, part * tile_rows : (part + 1) * tile_rows, part * pair :],
-                    pd_sem.at[head, part],
-                )
-                for part in range(tiles_dev)
-            ]
-            for head in range(groups)
-        ]
-        ins = [None] + [
-            pltpu.make_async_copy(pd_in_hbm.at[s], pd_in_ref.at[s], in_sem.at[s]) for s in range(1, devices)
-        ]
-        for copy in loads + [copy for row in owns for copy in row] + ins[1:]:
-            copy.start()
+        for load in loads:
+            load.start()
+        grad_ref[...] = jnp.zeros_like(grad_ref)
         more_ref[...] = jnp.zeros_like(more_ref)
-        for head in range(groups):
-            for part in range(1, tiles_dev, 2):
-                pd_ref[head, part * tile_rows : (part + 1) * tile_rows, (part - 1) * pair : part * pair] = jnp.zeros(
-                    (tile_rows, pair), jnp.bfloat16
-                )
-        for load in loads[:4]:
-            load.wait()
+        for part in range(1, tiles_dev, 2):
+            rows = slice(part * tile_rows, (part + 1) * tile_rows)
+            pd_ref[:, rows, (part - 1) * pair : part * pair] = jnp.zeros((groups, tile_rows, pair), jnp.bfloat16)
 
         lse_of = []
         gd_of = []
         for peer in range(devices):
-            table = back_ref[peer, base : base + 4 * devices, :].astype(jnp.float32)
+            table = back_ref[peer, base:, :].astype(jnp.float32)
             lse_of.append(table[:devices] + table[devices : 2 * devices])
-            gd_of.append(table[2 * devices : 3 * devices] + table[3 * devices :])
+            gd_of.append(table[2 * devices :])
             lse_sc[peer] = lse_of[peer]
             gd_sc[peer] = gd_of[peer]
 
         ids = lax.broadcasted_iota(jnp.int32, (devices, tile_rows), 0)
-        metas = [meta_ref[source].astype(jnp.float32) for source in range(devices)]
+        metas = [meta_ref[source] for source in range(devices)]
         rows_of = [
             jnp.concatenate([metas[source][entry : entry + 1] for source in range(devices)], axis=0).astype(jnp.int32)
             for entry in range(picked)
@@ -595,7 +556,40 @@
         d_sc[5] = -own_weight * stat_ref[2] * delta
         d_sc[6] = -own_weight * delta
 
-        loads[4].wait()
+        nothing = jnp.zeros((head_dim, tile_rows), jnp.bfloat16)
+        for source in range(1, devices):
+            odd = lax.rem(jnp.maximum(codes[source], 0), 2) == 1
+            first = w_sc[0, source : source + 1, :]
+            second = w_sc[1, source : source + 1, :]
+            turned = qgt_in_ref[source - 1].astype(jnp.float32)
+            g_first = (turned[head_dim:] * first).astype(jnp.bfloat16)
+            q_first = (turned[:head_dim] * first).astype(jnp.bfloat16)
+            q_second = (turned[:head_dim] * second).astype(jnp.bfloat16)
+            xin_ref[source, :head_dim, :tile_rows] = jnp.where(odd, q_second, g_first)
+            xin_ref[source, :head_dim, tile_rows:] = jnp.where(odd, q_first, nothing)
+            xin_ref[source, head_dim:, :tile_rows] = jnp.where(odd, g_first, q_second)
+            xin_ref[source, head_dim:, tile_rows:] = jnp.where(odd, nothing, q_first)
+        for source in range(1, devices):
+            head = lax.rem(jnp.maximum(codes[source], 0), groups)
+            target = grad_ref if source % 2 else more_ref
+            target[head] += dot_t(pd_in_ref[source - 1], xin_ref[source])
+
+        for load in loads:
+            load.wait()
+        for head in range(groups):
+            v_rows = slice(0, head_dim) if head % 2 == 0 else slice(head_dim, 2 * head_dim)
+            k_rows = slice(head_dim, 2 * head_dim) if head % 2 == 0 else slice(0, head_dim)
+            for tile in range(tiles_dev):
+                code = tile * groups + head
+                first = d_sc[4, code : code + 1, :]
+                second = d_sc[5, code : code + 1, :]
+                turned = qgt_ref[head, :, tile * tile_rows : (tile + 1) * tile_rows].astype(jnp.float32)
+                early = slice(tile * pair, tile * pair + tile_rows)
+                late = slice(tile * pair + tile_rows, (tile + 1) * pair)
+                x_ref[head, v_rows, early] = (turned[head_dim:] * first).astype(jnp.bfloat16)
+                x_ref[head, v_rows, late] = nothing
+                x_ref[head, k_rows, early] = (turned[:head_dim] * second).astype(jnp.bfloat16)
+                x_ref[head, k_rows, late] = (turned[:head_dim] * first).astype(jnp.bfloat16)
         for head in range(groups):
             for tile in range(tiles_dev):
                 code = tile * groups + head
@@ -640,43 +634,10 @@
         stores[0].start()
         stores[1].start()
 
-        for copy in loads[5:] + [copy for row in owns for copy in row] + ins[1:]:
-            copy.wait()
-        nothing = jnp.zeros((head_dim, tile_rows), jnp.bfloat16)
-        for head in range(groups):
-            v_rows = slice(0, head_dim) if head % 2 == 0 else slice(head_dim, 2 * head_dim)
-            k_rows = slice(head_dim, 2 * head_dim) if head % 2 == 0 else slice(0, head_dim)
-            for tile in range(tiles_dev):
-                code = tile * groups + head
-                first = d_sc[4, code : code + 1, :]
-                second = d_sc[5, code : code + 1, :]
-                turned = qgt_ref[head, :, tile * tile_rows : (tile + 1) * tile_rows].astype(jnp.float32)
-                early = slice(tile * pair, tile * pair + tile_rows)
-                late = slice(tile * pair + tile_rows, (tile + 1) * pair)
-                x_ref[head, v_rows, early] = (turned[head_dim:] * first).astype(jnp.bfloat16)
-                x_ref[head, v_rows, late] = nothing
-                x_ref[head, k_rows, early] = (turned[:head_dim] * second).astype(jnp.bfloat16)
-                x_ref[head, k_rows, late] = (turned[:head_dim] * first).astype(jnp.bfloat16)
-        for source in range(1, devices):
-            odd = lax.rem(jnp.maximum(codes[source], 0), 2) == 1
-            first = w_sc[0, source : source + 1, :]
-            second = w_sc[1, source : source + 1, :]
-            turned = qgt_in_ref[source].astype(jnp.float32)
-            g_first = (turned[head_dim:] * first).astype(jnp.bfloat16)
-            q_first = (turned[:head_dim] * first).astype(jnp.bfloat16)
-            q_second = (turned[:head_dim] * second).astype(jnp.bfloat16)
-            xin_ref[source, :head_dim, :tile_rows] = jnp.where(odd, q_second, g_first)
-            xin_ref[source, :head_dim, tile_rows:] = jnp.where(odd, q_first, nothing)
-            xin_ref[source, head_dim:, :tile_rows] = jnp.where(odd, g_first, q_second)
-            xin_ref[source, head_dim:, tile_rows:] = jnp.where(odd, nothing, q_first)
         for head in range(groups):
             for first in range(0, tiles_dev, 2):
                 rows = slice(first * tile_rows, (first + 2) * tile_rows)
-                grad_ref[head, rows, :] = dot_t(pd_ref[head, rows, first * pair :], x_ref[head, :, first * pair :])
-        for source in range(1, devices):
-            head = lax.rem(jnp.maximum(codes[source], 0), groups)
-            target = grad_ref if source % 2 else more_ref
-            target[head] += dot_t(pd_in_ref[source], xin_ref[source])
+                grad_ref[head, rows, :] += dot_t(pd_ref[head, rows, first * pair :], x_ref[head, :, first * pair :])
         lane = lax.broadcasted_iota(jnp.int32, (tile_rows, 2 * head_dim), 1)
         for head in range(0, groups, 2):
             cols = slice(head * head_dim, (head + 2) * head_dim)
@@ -711,12 +672,18 @@
     shape = jax.ShapeDtypeStruct
     dma = pltpu.SemaphoreType.DMA
     small = pltpu.CompilerParams(vmem_limit_bytes=vmem_grant)
-    large = pltpu.CompilerParams(vmem_limit_bytes=vmem_whole)
-    pair_cols = offsets_of(tiles_dev, tile_rows)[-1]
+    near = pltpu.VMEM
+
+    def away(*arrays):
+        return tuple(pltpu.with_memory_space_constraint(x, pltpu.HBM) for x in arrays)
+
+    def keep(*arrays):
+        return tuple(pltpu.with_memory_space_constraint(x, pltpu.VMEM) for x in arrays)
+
 
     send_q, task_of = pl.pallas_call(
         pack_kernel(tiles_dev, groups, picked, tile_rows, head_dim, devices),
-        out_shape=(shape((devices, tile_rows + 16, width), low), shape((devices,), jnp.int32)),
+        out_shape=(shape((devices, tile_rows + 8, width), low), shape((devices,), jnp.int32)),
         in_specs=[smem, vmem, vmem],
         out_specs=(vmem, smem),
         name="pack",
@@ -724,74 +691,67 @@
     recv_q = lax.all_to_all(send_q, "ctx", split_axis=0, concat_axis=0, tiled=True)
 
     mix_shape = (groups, tiles_dev, 3 * head_dim, tile_rows)
-    pair_shape = (groups, tile_rows, pair_cols)
-    kv, vkt, qgt, stats, table, mix, pairs = pl.pallas_call(
+    pair_shape = (groups, row_count, 2 * row_count)
+    kv, vkt, stats, table, qgt, mix, pairs = pl.pallas_call(
         own_kernel(tiles_dev, groups, tile_rows, head_dim, devices),
         out_shape=(
-            shape((groups, row_count, width), low),
-            shape((groups, width, row_count), low),
-            shape((groups, width, row_count), low),
-            shape((3, tasks, tile_rows), wide),
-            shape((tasks, 4 * devices, tile_rows), wide),
-            shape(mix_shape, low),
-            shape(pair_shape, low),
+            near((groups, row_count, width), low),
+            near((groups, width, row_count), low),
+            near((3, tasks, tile_rows), wide),
+            near((tasks, 8, tile_rows), wide),
+            pltpu.HBM((groups, width, row_count), low),
+            pltpu.HBM(mix_shape, low),
+            pltpu.HBM(pair_shape, low),
         ),
         in_specs=[far] * 4,
-        out_specs=(vmem, vmem, vmem, vmem, vmem, far, far),
+        out_specs=tuple([vmem] * 4 + [far] * 3),
         scratch_shapes=[pltpu.VMEM((row_count, columns), low)] * 4
-        + [pltpu.VMEM(mix_shape, low), pltpu.VMEM(pair_shape, low), dma((4,)), dma((2, groups))],
-        compiler_params=large,
+        + [
+            pltpu.VMEM((groups, width, row_count), low),
+            pltpu.VMEM(mix_shape, low),
+            pltpu.VMEM(pair_shape, low),
+            dma((4,)),
+            dma((tiles_dev + 2,)),
+        ],
+        compiler_params=small,
         name="own",
-    )(query, key, value, grad_out)
-
-    slot = 3 * head_dim + 4 * devices
-    in_shape = (devices, row_count, 2 * tile_rows)
+    )(*away(query, key, value, grad_out))
+
+    slot = 3 * head_dim + 3 * devices
+    in_shape = (devices - 1, row_count, 2 * tile_rows)
     send_b, inverse_in = pl.pallas_call(
         serve_kernel(groups, tile_rows, head_dim, devices),
-        out_shape=(shape((devices, slot, tile_rows), low), shape((devices, tile_rows), wide)),
-        in_specs=[smem, smem, far, far, far, far],
-        out_specs=(far, far),
+        out_shape=(pltpu.HBM((devices, slot, tile_rows), low), near((devices, tile_rows), wide)),
+        in_specs=[smem, smem, vmem, vmem, vmem, vmem],
+        out_specs=(far, vmem),
         scratch_shapes=[
             pltpu.VMEM((devices, slot, tile_rows), low),
-            pltpu.VMEM((devices, tile_rows), wide),
-            pltpu.VMEM((4 * devices, tile_rows), wide),
-            pltpu.VMEM(send_q.shape, low),
-            pltpu.VMEM(kv.shape, low),
-            pltpu.VMEM(vkt.shape, low),
-            pltpu.VMEM(table.shape, wide),
-            dma((4,)),
-            dma((2,)),
+            pltpu.VMEM((3 * devices, tile_rows), wide),
+            dma(()),
         ],
         compiler_params=small,
         name="serve",
-    )(picks, task_of, recv_q, kv, vkt, table)
+    )(*away(picks, task_of), *keep(recv_q, kv, vkt, table))
     recv_b = lax.all_to_all(send_b, "ctx", split_axis=0, concat_axis=0, tiled=True)
 
-    pairs_in, qgt_in = pl.pallas_call(
+    pairs_in, qgt_in, lists_in = pl.pallas_call(
         again_kernel(groups, tile_rows, head_dim, devices),
-        out_shape=(shape(in_shape, low), shape((devices, width, tile_rows), low)),
+        out_shape=(near(in_shape, low), near((devices - 1, width, tile_rows), low), near((devices, 8, width), wide)),
         in_specs=[smem, vmem, vmem],
-        out_specs=(vmem, vmem),
-        compiler_params=large,
+        out_specs=(vmem, vmem, vmem),
+        compiler_params=small,
         name="again",
-    )(picks, recv_q, kv)
-
-    square = (groups, row_count, 2 * row_count)
+    )(*away(picks), *keep(recv_q, kv))
+
     return pl.pallas_call(
         final_kernel(tiles_dev, groups, picked, tile_rows, head_dim, devices),
         out_shape=tuple([shape((row_count, columns), low)] * 4),
-        in_specs=[smem, smem] + [far] * 9,
+        in_specs=[smem, smem] + [vmem] * 6 + [far] * 3,
         out_specs=tuple([far] * 4),
         scratch_shapes=[
-            pltpu.VMEM((devices, 16, width), low),
-            pltpu.VMEM((devices, slot, tile_rows), low),
-            pltpu.VMEM(qgt.shape, low),
-            pltpu.VMEM(qgt_in.shape, low),
-            pltpu.VMEM(stats.shape, wide),
-            pltpu.VMEM(inverse_in.shape, wide),
+            pltpu.VMEM((groups, width, row_count), low),
             pltpu.VMEM(mix_shape, low),
-            pltpu.VMEM(in_shape, low),
-            pltpu.VMEM(square, low),
+            pltpu.VMEM(pair_shape, low),
         ]
         + [pltpu.VMEM((row_count, columns), low)] * 4
         + [
@@ -804,14 +764,12 @@
             pltpu.VMEM((7, tasks, tile_rows), wide),
             pltpu.VMEM((groups, width, 2 * row_count), low),
             pltpu.VMEM((devices, width, 2 * tile_rows), low),
-            dma((7,)),
-            dma((groups, tiles_dev)),
-            dma((devices,)),
+            dma((tiles_dev + 2,)),
             dma((4,)),
         ],
         compiler_params=small,
         name="final",
-    )(picks, task_of, recv_q, recv_b, qgt, qgt_in, stats, inverse_in, mix, pairs_in, pairs)
+    )(*away(picks, task_of), *keep(lists_in, recv_b, qgt_in, stats, inverse_in, pairs_in), *away(qgt, mix, pairs))
 
 
 def choose(query, key, value, grad_out, picks):

time: 49 us -> 45.7 us (0.933)
  Pallas kernels: 27.3 us -> 22.8 us
  waiting for transfers between devices: 8.76 us -> 9.67 us
    pallas_call x1, Pallas kernels: 5.43 us -> 3.73 us  [fast_local(): pl.pallas_call(again_kernel(groups, tile_rows, head_dim, devices), out_sh...]
    pallas_call x1, Pallas kernels: 4.72 us -> 3.33 us  [fast_local(): pl.pallas_call(serve_kernel(groups, tile_rows, head_dim, devices), out_sh...]
    pallas_call x1, Pallas kernels: 6.87 us -> 5.54 us  [fast_local(): pl.pallas_call(final_kernel(tiles_dev, groups, picked, tile_rows, head_di...]
    all_to_all x1, waiting for transfers between devices: 7.24 us -> 8.47 us  [fast_local(): lax.all_to_all(send_b, 'ctx', split_axis=0, concat_axis=0, tiled=True)]
  transfers between devices with their start and end apart: 2 -> 2, of which waited for: 2 -> 2; matrix products, arithmetic and copies ran while one was open for 0% -> 0% of each run, Pallas kernels for 28% -> 26%
where the time goes in v3:
time: 45.7 us; the launch traced here: 45.2 us
  Pallas kernels  22.8 us (50%)
  starting transfers between devices  12.1 us (26%)
  waiting for transfers between devices  9.67 us (21%)
  between operations  0.66 us (1%)
    all_to_all x1, waiting for transfers between devices, fast_local(): lax.all_to_all(send_b, 'ctx', split_axis=0, concat_axis=0, tiled=True)  8.47 us
    pallas_call x1, Pallas kernels, fast_local(): pl.pallas_call(own_kernel(tiles_dev, groups, tile_rows, head_dim, devices...  8.06 us
    all_to_all x1, starting transfers between devices, fast_local(): lax.all_to_all(send_q, 'ctx', split_axis=0, concat_axis=0, tiled=True)  7.29 us
    pallas_call x1, Pallas kernels, fast_local(): pl.pallas_call(final_kernel(tiles_dev, groups, picked, tile_rows, head_di...  5.54 us
    all_to_all x1, starting transfers between devices, fast_local(): lax.all_to_all(send_b, 'ctx', split_axis=0, concat_axis=0, tiled=True)  4.83 us
    pallas_call x1, Pallas kernels, fast_local(): pl.pallas_call(again_kernel(groups, tile_rows, head_dim, devices), out_sh...  3.73 us
    pallas_call x1, Pallas kernels, fast_local(): pl.pallas_call(serve_kernel(groups, tile_rows, head_dim, devices), out_sh...  3.33 us
    pallas_call x1, Pallas kernels, fast_local(): pl.pallas_call(pack_kernel(tiles_dev, groups, picked, tile_rows, head_dim...  2.08 us
  transfers between devices with their start and end apart: 2, of which 2 were waited for; matrix products, arithmetic and copies ran while one was open for 0% of the time, Pallas kernels for 26%

profile of v3, /device:TPU:0, one launch (start us, length us, event | category | flops | bytes accessed | tf_op | source)
XLA Modules:
  0.0 45.2 jit_solution(15579981312571398598)
XLA Ops:
  0.6 2.1 %pack.1 = (bf16[8,136,128]{2,1,0:T(8,128)(2,1)}, s32[8]{0:T(128)}) custom-call(s32[4,4,4]{2,1,0:T(4,128)} %picks_ref.7, bf16[512,256]{1,0:T(8,128)(2,1)} %q_hbm.1, bf16[512,256]{1,0:T(8,128)(2,1)} %g_hbm.1), custom_call_target="tpu_custom_call" | custom-call | tf_op jit(solution)/shard_map/pack/pallas_call | solution.py:684
  2.7 7.3 %all-to-all-start = ((bf16[8,136,128]{2,1,0:T(8,128)(2,1)}), bf16[8,136,128]{2,1,0:T(8,128)(2,1)S(1)}, u32[]{:S(2)}, u32[]{:S(2)}) async-start(bf16[8,136,128]{2,1,0:T(8,128)(2,1)} %get-tuple-element.19), calls=%async_computation | async-start | bytes 557056 | tf_op jit(solution)/shard_map/all_to_all | solution.py:691
  10.0 8.1 %own.1 = (bf16[4,512,128]{2,1,0:T(8,128)(2,1)S(1)}, bf16[4,128,512]{2,1,0:T(8,128)(2,1)S(1)}, f32[3,16,128]{2,1,0:T(8,128)S(1)}, f32[16,8,128]{2,1,0:T(8,128)S(1...) custom-call(bf16[512,256]{1,0:T(8,128)(2,1)} %q_hbm.1, ...), custom_call_target="tpu_custom_call" | custom-call | tf_op jit(solution)/shard_map/own/pallas_call | solution.py:695
  18.1 1.2 %all-to-all-done.recv_ref = bf16[8,136,128]{2,1,0:T(8,128)(2,1)S(1)} async-done(((bf16[8,136,128]{2,1,0:T(8,128)(2,1)}), bf16[8,136,128]{2,1,0:T(8,128)(2,1)S(1)}, u32[]{:S(2)}, u32[]{:S(2)}) %all-to-all-start) | async-done | bytes 278560 | tf_op jit(solution)/shard_map/all_to_all | solution.py:691
  19.3 3.3 %serve.1 = (bf16[8,216,128]{2,1,0:T(8,128)(2,1)}, f32[8,128]{1,0:T(8,128)S(1)}) custom-call(s32[4,4,4]{2,1,0:T(4,128)} %picks_ref.7, s32[8]{0:T(128)} %get-tuple-element.18.task_ref, bf16[8,136,128]{2,1,0:T(8,128)(2,1)S(1)} %all-to-all-done.recv_ref, bf16[4,512,128]{2,1,0:T(8,128)(2,1)S(1)} %get-tuple-element.20.kv_ref, ...), custom_call_target="tpu_custom_call" | custom-call | tf_op jit(solution)/shard_map/serve/pallas_call | solution.py:722
  22.6 4.8 %all-to-all-start.1 = ((bf16[8,216,128]{2,1,0:T(8,128)(2,1)}), bf16[8,216,128]{2,1,0:T(8,128)(2,1)S(1)}, u32[]{:S(2)}, u32[]{:S(2)}) async-start(bf16[8,216,128]{2,1,0:T(8,128)(2,1)} %get-tuple-element.24), calls=%async_computation.1 | async-start | bytes 884736 | tf_op jit(solution)/shard_map/all_to_all | solution.py:735
  27.4 3.7 %again.1 = (bf16[7,512,256]{2,1,0:T(8,128)(2,1)S(1)}, bf16[7,128,128]{2,1,0:T(8,128)(2,1)S(1)}, f32[8,8,128]{2,1,0:T(8,128)S(1)}) custom-call(s32[4,4,4]{2,1,0:T(4,128)} %picks_ref.7, bf16[8,136,128]{2,1,0:T(8,128)(2,1)S(1)} %all-to-all-done.recv_ref, bf16[4,512,128]{2,1,0:T(8,128)(2,1)S(1)} %get-tuple-element.20.kv_ref), custom_call_target="tpu_custom_call" | custom-call | tf_op jit(solution)/shard_map/again/pallas_call | solution.py:737
  31.2 8.5 %all-to-all-done.1.back_ref = bf16[8,216,128]{2,1,0:T(8,128)(2,1)S(1)} async-done(((bf16[8,216,128]{2,1,0:T(8,128)(2,1)}), bf16[8,216,128]{2,1,0:T(8,128)(2,1)S(1)}, u32[]{:S(2)}, u32[]{:S(2)}) %all-to-all-start.1) | async-done | bytes 442400 | tf_op jit(solution)/shard_map/all_to_all | solution.py:735
  39.7 5.5 %final.1 = (bf16[512,256]{1,0:T(8,128)(2,1)}, bf16[512,256]{1,0:T(8,128)(2,1)}, bf16[512,256]{1,0:T(8,128)(2,1)}, bf16[512,256]{1,0:T(8,128)(2,1)}) custom-call(s32[4,4,4]{2,1,0:T(4,128)} %picks_ref.7, s32[8]{0:T(128)} %get-tuple-element.18.task_ref, f32[8,8,128]{2,1,0:T(8,128)S(1)} %get-tuple-element.21.meta_ref, ...), custom_call_target="tpu_custom_call" | custom-call | tf_op jit(solution)/shard_map/final/pallas_call | solution.py:746
Async XLA Ops:
  2.7 16.6 %all-to-all-start = ((bf16[8,136,128]{2,1,0:T(8,128)(2,1)}), bf16[8,136,128]{2,1,0:T(8,128)(2,1)S(1)}, u32[]{:S(2)}, u32[]{:S(2)}) async-start(bf16[8,136,128]{2,1,0:T(8,128)(2,1)} %get-tuple-element.19), calls=%async_computation | async-start | bytes 557056 | tf_op jit(solution)/shard_map/all_to_all | solution.py:691
  22.6 17.0 %all-to-all-start.1 = ((bf16[8,216,128]{2,1,0:T(8,128)(2,1)}), bf16[8,216,128]{2,1,0:T(8,128)(2,1)S(1)}, u32[]{:S(2)}, u32[]{:S(2)}) async-start(bf16[8,216,128]{2,1,0:T(8,128)(2,1)} %get-tuple-element.24), calls=%async_computation.1 | async-start | bytes 884736 | tf_op jit(solution)/shard_map/all_to_all | solution.py:735

commit v4 on v3

--- a/solution.py
+++ b/solution.py
@@ -308,11 +308,11 @@
     return body
 
 
-def own_kernel(tiles_dev, groups, tile_rows, head_dim, devices):
+def own_kernel(tiles_dev, groups, tile_rows, head_dim):
     scale = LOG2E / math.sqrt(head_dim)
 
-    def body(q_hbm, k_hbm, v_hbm, g_hbm, kv_ref, vkt_ref, stat_ref, table_ref, qgt_hbm, mix_hbm,
-             pd_hbm, q_ref, k_ref, v_ref, g_ref, qgt_ref, mix_ref, pd_ref, in_sem, out_sem):
+    def body(q_hbm, k_hbm, v_hbm, g_hbm, kv_ref, vkt_ref, stat_ref, table_ref,
+             q_ref, k_ref, v_ref, g_ref, in_sem):
         loads = [
             pltpu.make_async_copy(src, dst, in_sem.at[index])
             for index, (src, dst) in enumerate(((k_hbm, k_ref), (v_hbm, v_ref), (q_hbm, q_ref), (g_hbm, g_ref)))
@@ -326,50 +326,96 @@
         causal = sub <= lane
         for head in range(groups):
             cols = slice(head * head_dim, (head + 1) * head_dim)
-            k_head = k_ref[:, cols]
-            v_head = v_ref[:, cols]
-            kv_ref[head] = jnp.concatenate([k_head, v_head], axis=1)
-            vkt_ref[head] = jnp.concatenate([v_head, k_head], axis=1).T
-            block_all = jnp.concatenate([q_ref[:, cols], g_ref[:, cols]], axis=1)
-            qgt_ref[head] = block_all.T
-            for tile in range(tiles_dev):
-                rows = slice(tile * tile_rows, (tile + 1) * tile_rows)
-                span = (tile + 1) * tile_rows
-                code = tile * groups + head
-                at = tile * 2 * tile_rows
-                both = dot_t(kv_ref[head, :span, :], jnp.concatenate(halves(block_all[rows], head_dim), axis=0))
-                scores = both[:, :tile_rows]
-                last = jnp.where(causal, scores[span - tile_rows :], masked_value)
-                peak = jnp.max(last, axis=0, keepdims=True)
-                if tile:
-                    peak = jnp.maximum(peak, jnp.max(scores[: span - tile_rows], axis=0, keepdims=True))
-                peak = peak * scale
-                total = jnp.zeros((1, tile_rows), jnp.float32)
-                mean_grad = jnp.zeros((1, tile_rows), jnp.float32)
-                for part in range(tile + 1):
-                    chunk = slice(part * tile_rows, (part + 1) * tile_rows)
-                    piece = last if part == tile else scores[chunk]
-                    powers = jnp.exp2(piece * scale - peak)
-                    spread = powers * both[chunk, tile_rows:]
-                    total = total + jnp.sum(powers, axis=0, keepdims=True)
-                    mean_grad = mean_grad + jnp.sum(spread, axis=0, keepdims=True)
-                    pd_ref[head, chunk, at : at + tile_rows] = powers.astype(jnp.bfloat16)
-                    pd_ref[head, chunk, at + tile_rows : at + 2 * tile_rows] = spread.astype(jnp.bfloat16)
-                inverse = 1.0 / total
-                mean_grad = mean_grad * inverse
-                lse = peak + jnp.log2(total)
-                result = jnp.dot(vkt_ref[head, :, :span], pd_ref[head, :span, at : at + 2 * tile_rows],
-                                 preferred_element_type=jnp.float32)
-                top = result[:, :tile_rows]
-                low = result[head_dim:, tile_rows:]
-                mix_ref[head, tile, : 2 * head_dim, :] = (top * inverse).astype(jnp.bfloat16)
-                mix_ref[head, tile, 2 * head_dim :, :] = (low * inverse).astype(jnp.bfloat16)
-                stat_ref[0, code : code + 1, :] = lse
-                stat_ref[1, code : code + 1, :] = mean_grad
-                stat_ref[2, code : code + 1, :] = inverse
-                parts = split_low(lse) + (mean_grad,)
-                for index in range(3):
-                    table_ref[code, index : index + 1, :] = parts[index]
+            kv_ref[head] = jnp.concatenate([k_ref[:, cols], v_ref[:, cols]], axis=1)
+
+        def product(code):
+            tile, head = code // groups, code % groups
+            cols = slice(head * head_dim, (head + 1) * head_dim)
+            rows = slice(tile * tile_rows, (tile + 1) * tile_rows)
+            block = jnp.concatenate([q_ref[rows, cols], g_ref[rows, cols]], axis=1)
+            return dot_t(kv_ref[head, : rows.stop, :], jnp.concatenate(halves(block, head_dim), axis=0))
+
+        ahead = product(0)
+        for code in range(tiles_dev * groups):
+            both = ahead
+            if code + 1 < tiles_dev * groups:
+                ahead = product(code + 1)
+            tile = code // groups
+            split = tile * tile_rows
+            last = jnp.where(causal, both[split:, :tile_rows], masked_value)
+            peak = jnp.max(last, axis=0, keepdims=True)
+            if tile:
+                peak = jnp.maximum(peak, jnp.max(both[:split, :tile_rows], axis=0, keepdims=True))
+            peak = peak * scale
+            powers = jnp.exp2(last * scale - peak)
+            total = jnp.sum(powers, axis=0, keepdims=True)
+            mean_grad = jnp.sum(powers * both[split:, tile_rows:], axis=0, keepdims=True)
+            if tile:
+                powers = jnp.exp2(both[:split, :tile_rows] * scale - peak)
+                total = total + jnp.sum(powers, axis=0, keepdims=True)
+                mean_grad = mean_grad + jnp.sum(powers * both[:split, tile_rows:], axis=0, keepdims=True)
+            inverse = 1.0 / total
+            mean_grad = mean_grad * inverse
+            lse = peak + jnp.log2(total)
+            for index, value in enumerate((lse, mean_grad, inverse, peak)):
+                stat_ref[index, code : code + 1, :] = value
+            for index, value in enumerate(split_low(lse) + (mean_grad,)):
+                table_ref[code, index : index + 1, :] = value
+        for head in range(groups):
+            cols = slice(head * head_dim, (head + 1) * head_dim)
+            vkt_ref[head] = jnp.concatenate([v_ref[:, cols], k_ref[:, cols]], axis=1).T
+
+    return body
+
+
+def rest_kernel(tiles_dev, groups, tile_rows, head_dim):
+    scale = LOG2E / math.sqrt(head_dim)
+
+    def body(q_hbm, g_hbm, kv_ref, vkt_ref, stat_ref, qgt_hbm, mix_hbm, pd_hbm,
+             q_ref, g_ref, qgt_ref, mix_ref, pd_ref, in_sem, out_sem):
+        loads = [
+            pltpu.make_async_copy(src, dst, in_sem.at[index])
+            for index, (src, dst) in enumerate(((q_hbm, q_ref), (g_hbm, g_ref)))
+        ]
+        for load in loads:
+            load.start()
+        for load in loads:
+            load.wait()
+        sub = lax.broadcasted_iota(jnp.int32, (tile_rows, tile_rows), 0)
+        lane = lax.broadcasted_iota(jnp.int32, (tile_rows, tile_rows), 1)
+        causal = sub <= lane
+
+        def product(code):
+            tile, head = code // groups, code % groups
+            cols = slice(head * head_dim, (head + 1) * head_dim)
+            rows = slice(tile * tile_rows, (tile + 1) * tile_rows)
+            block = jnp.concatenate([q_ref[rows, cols], g_ref[rows, cols]], axis=1)
+            qgt_ref[head, :, rows] = block.T
+            return dot_t(kv_ref[head, : rows.stop, :], jnp.concatenate(halves(block, head_dim), axis=0))
+
+        ahead = product(0)
+        for code in range(tiles_dev * groups):
+            both = ahead
+            if code + 1 < tiles_dev * groups:
+                ahead = product(code + 1)
+            tile, head = code // groups, code % groups
+            span = (tile + 1) * tile_rows
+            at = tile * 2 * tile_rows
+            peak = stat_ref[3, code : code + 1, :]
+            inverse = stat_ref[2, code : code + 1, :]
+            for part in range(tile + 1):
+                chunk = slice(part * tile_rows, (part + 1) * tile_rows)
+                scores = both[chunk, :tile_rows]
+                if part == tile:
+                    scores = jnp.where(causal, scores, masked_value)
+                powers = jnp.exp2(scores * scale - peak)
+                spread = powers * both[chunk, tile_rows:]
+                pd_ref[head, chunk, at : at + tile_rows] = powers.astype(jnp.bfloat16)
+                pd_ref[head, chunk, at + tile_rows : at + 2 * tile_rows] = spread.astype(jnp.bfloat16)
+            result = jnp.dot(vkt_ref[head, :, :span], pd_ref[head, :span, at : at + 2 * tile_rows],
+                             preferred_element_type=jnp.float32)
+            mix_ref[head, tile, : 2 * head_dim, :] = (result[:, :tile_rows] * inverse).astype(jnp.bfloat16)
+            mix_ref[head, tile, 2 * head_dim :, :] = (result[head_dim:, tile_rows:] * inverse).astype(jnp.bfloat16)
         stores = [
             pltpu.make_async_copy(mix_ref, mix_hbm, out_sem.at[tiles_dev]),
             pltpu.make_async_copy(qgt_ref, qgt_hbm, out_sem.at[tiles_dev + 1]),
@@ -424,7 +470,8 @@
             parts = split_low(peak + jnp.log2(total)) + (mean_grad,)
             for index in range(3):
                 st_ref[index * devices + source : index * devices + source + 1, :] = parts[index]
-            inv_ref[source : source + 1, :] = inverse
+            inv_ref[0, source : source + 1, :] = inverse
+            inv_ref[1, source : source + 1, :] = peak
         table = st_ref[...]
         row = lax.broadcasted_iota(jnp.int32, table.shape, 0)
         mine = lax.rem(row, devices) == own
@@ -445,23 +492,28 @@
 def again_kernel(groups, tile_rows, head_dim, devices):
     scale = LOG2E / math.sqrt(head_dim)
 
-    def body(picks_ref, recv_ref, kv_ref, pd_ref, qgt_ref, meta_ref):
+    def body(picks_ref, recv_ref, kv_ref, inv_ref, pd_ref, qgt_ref, meta_ref):
         own = picks_ref[0, 0, 0]
         for source in range(devices):
             meta_ref[source] = recv_ref[source, tile_rows:, :].astype(jnp.float32)
-
-        def turn(source, carry):
-            code = jnp.max(recv_ref[source, tile_rows:, :].astype(jnp.float32)[0:1, :]).astype(jnp.int32) - 1
+        codes = [jnp.max(recv_ref[source, tile_rows:, :].astype(jnp.float32)[0:1, :]).astype(jnp.int32) - 1
+                 for source in range(devices)]
+
+        def product(source):
             block = recv_ref[source, :tile_rows, :]
-            block = jnp.where((code >= 0) & (own != source), block, jnp.zeros_like(block))
-            head = lax.rem(jnp.maximum(code, 0), groups)
-            _, powers, spread = parts_of(block, kv_ref[head], tile_rows, head_dim, scale)
+            block = jnp.where((codes[source] >= 0) & (own != source), block, jnp.zeros_like(block))
+            qgt_ref[source - 1] = block.T
+            head = lax.rem(jnp.maximum(codes[source], 0), groups)
+            return dot_t(kv_ref[head], jnp.concatenate(halves(block, head_dim), axis=0))
+
+        ahead = product(1)
+        for source in range(1, devices):
+            both = ahead
+            if source + 1 < devices:
+                ahead = product(source + 1)
+            powers = jnp.exp2(both[:, :tile_rows] * scale - inv_ref[1, source : source + 1, :])
             pd_ref[source - 1, :, :tile_rows] = powers.astype(jnp.bfloat16)
-            pd_ref[source - 1, :, tile_rows:] = spread.astype(jnp.bfloat16)
-            qgt_ref[source - 1] = block.T
-            return carry
-
-        lax.fori_loop(1, devices, turn, 0)
+            pd_ref[source - 1, :, tile_rows:] = (powers * both[:, tile_rows:]).astype(jnp.bfloat16)
 
     return body
 
@@ -525,7 +577,7 @@
             total = total + power
             delta = delta + jnp.where(chosen[peer], power * gd_of[peer], 0.0)
         delta = delta / total
-        weight = jnp.exp2(lse_sc[own] - peak) / total * inv_ref[...]
+        weight = jnp.exp2(lse_sc[own] - peak) / total * inv_ref[0]
         w_sc[0] = jnp.where(live, weight, 0.0)
         w_sc[1] = jnp.where(live, -weight * delta, 0.0)
 
@@ -574,7 +626,7 @@
             target = grad_ref if source % 2 else more_ref
             target[head] += dot_t(pd_in_ref[source - 1], xin_ref[source])
 
-        for load in loads:
+        for load in loads[:2]:
             load.wait()
         for head in range(groups):
             v_rows = slice(0, head_dim) if head % 2 == 0 else slice(head_dim, 2 * head_dim)
@@ -634,17 +686,20 @@
         stores[0].start()
         stores[1].start()
 
-        for head in range(groups):
+        for load in loads[2:]:
+            load.wait()
+        half = 2 * tile_rows
+        lane = lax.broadcasted_iota(jnp.int32, (half, 2 * head_dim), 1)
+        for head in range(0, groups, 2):
+            cols = slice(head * head_dim, (head + 2) * head_dim)
             for first in range(0, tiles_dev, 2):
                 rows = slice(first * tile_rows, (first + 2) * tile_rows)
-                grad_ref[head, rows, :] += dot_t(pd_ref[head, rows, first * pair :], x_ref[head, :, first * pair :])
-        lane = lax.broadcasted_iota(jnp.int32, (tile_rows, 2 * head_dim), 1)
-        for head in range(0, groups, 2):
-            cols = slice(head * head_dim, (head + 2) * head_dim)
-            for part in range(tiles_dev):
-                rows = slice(part * tile_rows, (part + 1) * tile_rows)
-                even = grad_ref[head, rows, :] + more_ref[head, rows, :]
-                odd = grad_ref[head + 1, rows, :] + more_ref[head + 1, rows, :]
+                even, odd = (
+                    dot_t(pd_ref[h, rows, first * pair :], x_ref[h, :, first * pair :])
+                    + grad_ref[h, rows, :]
+                    + more_ref[h, rows, :]
+                    for h in (head, head + 1)
+                )
                 dv_ref[rows, cols] = jnp.where(lane < head_dim, even, odd).astype(jnp.bfloat16)
                 swapped = jnp.where(lane < head_dim, odd, even) * scaling
                 dk_ref[rows, cols] = pltpu.roll(swapped, head_dim, 1).astype(jnp.bfloat16)
@@ -690,29 +745,17 @@
     )(picks, query, grad_out)
     recv_q = lax.all_to_all(send_q, "ctx", split_axis=0, concat_axis=0, tiled=True)
 
-    mix_shape = (groups, tiles_dev, 3 * head_dim, tile_rows)
-    pair_shape = (groups, row_count, 2 * row_count)
-    kv, vkt, stats, table, qgt, mix, pairs = pl.pallas_call(
-        own_kernel(tiles_dev, groups, tile_rows, head_dim, devices),
+    kv, vkt, stats, table = pl.pallas_call(
+        own_kernel(tiles_dev, groups, tile_rows, head_dim),
         out_shape=(
             near((groups, row_count, width), low),
             near((groups, width, row_count), low),
-            near((3, tasks, tile_rows), wide),
+            near((4, tasks, tile_rows), wide),
             near((tasks, 8, tile_rows), wide),
-            pltpu.HBM((groups, width, row_count), low),
-            pltpu.HBM(mix_shape, low),
-            pltpu.HBM(pair_shape, low),
         ),
         in_specs=[far] * 4,
-        out_specs=tuple([vmem] * 4 + [far] * 3),
-        scratch_shapes=[pltpu.VMEM((row_count, columns), low)] * 4
-        + [
-            pltpu.VMEM((groups, width, row_count), low),
-            pltpu.VMEM(mix_shape, low),
-            pltpu.VMEM(pair_shape, low),
-            dma((4,)),
-            dma((tiles_dev + 2,)),
-        ],
+        out_specs=tuple([vmem] * 4),
+        scratch_shapes=[pltpu.VMEM((row_count, columns), low)] * 4 + [dma((4,))],
         compiler_params=small,
         name="own",
     )(*away(query, key, value, grad_out))
@@ -721,7 +764,7 @@
     in_shape = (devices - 1, row_count, 2 * tile_rows)
     send_b, inverse_in = pl.pallas_call(
         serve_kernel(groups, tile_rows, head_dim, devices),
-        out_shape=(pltpu.HBM((devices, slot, tile_rows), low), near((devices, tile_rows), wide)),
+        out_shape=(pltpu.HBM((devices, slot, tile_rows), low), near((2, devices, tile_rows), wide)),
         in_specs=[smem, smem, vmem, vmem, vmem, vmem],
         out_specs=(far, vmem),
         scratch_shapes=[
@@ -737,11 +780,31 @@
     pairs_in, qgt_in, lists_in = pl.pallas_call(
         again_kernel(groups, tile_rows, head_dim, devices),
         out_shape=(near(in_shape, low), near((devices - 1, width, tile_rows), low), near((devices, 8, width), wide)),
-        in_specs=[smem, vmem, vmem],
+        in_specs=[smem, vmem, vmem, vmem],
         out_specs=(vmem, vmem, vmem),
         compiler_params=small,
         name="again",
-    )(*away(picks), *keep(recv_q, kv))
+    )(*away(picks), *keep(recv_q, kv, inverse_in))
+
+    mix_shape = (groups, tiles_dev, 3 * head_dim, tile_rows)
+    pair_shape = (groups, row_count, 2 * row_count)
+    turned_shape = (groups, width, row_count)
+    qgt, mix, pairs = pl.pallas_call(
+        rest_kernel(tiles_dev, groups, tile_rows, head_dim),
+        out_shape=(pltpu.HBM(turned_shape, low), pltpu.HBM(mix_shape, low), pltpu.HBM(pair_shape, low)),
+        in_specs=[far] * 2 + [vmem] * 3,
+        out_specs=tuple([far] * 3),
+        scratch_shapes=[pltpu.VMEM((row_count, columns), low)] * 2
+        + [
+            pltpu.VMEM(turned_shape, low),
+            pltpu.VMEM(mix_shape, low),
+            pltpu.VMEM(pair_shape, low),
+            dma((2,)),
+            dma((tiles_dev + 2,)),
+        ],
+        compiler_params=small,
+        name="rest",
+    )(*away(query, grad_out), *keep(kv, vkt, stats))
 
     return pl.pallas_call(
         final_kernel(tiles_dev, groups, picked, tile_rows, head_dim, devices),

time: 45.7 us -> 43.9 us (0.961)
  Pallas kernels: 22.8 us -> 20.1 us
  waiting for transfers between devices: 9.67 us -> 11.7 us
  starting transfers between devices: 12.1 us -> 10.9 us
    all_to_all x1, waiting for transfers between devices: 1.19 us -> 6.58 us  [fast_local(): lax.all_to_all(send_q, 'ctx', split_axis=0, concat_axis=0, tiled=True)]
    all_to_all x1, waiting for transfers between devices: 8.47 us -> 5.15 us  [fast_local(): lax.all_to_all(send_b, 'ctx', split_axis=0, concat_axis=0, tiled=True)]
    pallas_call x1, Pallas kernels: 3.73 us -> 1.57 us  [fast_local(): pl.pallas_call(again_kernel(groups, tile_rows, head_dim, devices), out_sh...]
    all_to_all x1, starting transfers between devices: 4.83 us -> 3.6 us  [fast_local(): lax.all_to_all(send_b, 'ctx', split_axis=0, concat_axis=0, tiled=True)]
    pallas_call x1, Pallas kernels: 5.54 us -> 4.82 us  [fast_local(): pl.pallas_call(final_kernel(tiles_dev, groups, picked, tile_rows, head_di...]
    pallas_call x1 -> x2, Pallas kernels: 8.06 us -> 8.33 us  [the longest x1 5.66 us: fast_local(): pl.pallas_call(rest_kernel(tiles_dev, groups, tile_rows, head_dim), out_s...]
  transfers between devices with their start and end apart: 2 -> 2, of which waited for: 2 -> 2; matrix products, arithmetic and copies ran while one was open for 0% -> 0% of each run, Pallas kernels for 26% -> 23%
where the time goes in v4:
time: 43.9 us; the launch traced here: 43.4 us
  Pallas kernels  20.1 us (46%)
  waiting for transfers between devices  11.7 us (27%)
  starting transfers between devices  10.9 us (25%)
  between operations  0.67 us (2%)
    all_to_all x1, starting transfers between devices, fast_local(): lax.all_to_all(send_q, 'ctx', split_axis=0, concat_axis=0, tiled=True)  7.29 us
    all_to_all x1, waiting for transfers between devices, fast_local(): lax.all_to_all(send_q, 'ctx', split_axis=0, concat_axis=0, tiled=True)  6.58 us
    pallas_call x1, Pallas kernels, fast_local(): pl.pallas_call(rest_kernel(tiles_dev, groups, tile_rows, head_dim), out_s...  5.66 us
    all_to_all x1, waiting for transfers between devices, fast_local(): lax.all_to_all(send_b, 'ctx', split_axis=0, concat_axis=0, tiled=True)  5.15 us
    pallas_call x1, Pallas kernels, fast_local(): pl.pallas_call(final_kernel(tiles_dev, groups, picked, tile_rows, head_di...  4.82 us
    all_to_all x1, starting transfers between devices, fast_local(): lax.all_to_all(send_b, 'ctx', split_axis=0, concat_axis=0, tiled=True)  3.6 us
    pallas_call x1, Pallas kernels, fast_local(): pl.pallas_call(serve_kernel(groups, tile_rows, head_dim, devices), out_sh...  3.32 us
    pallas_call x1, Pallas kernels, fast_local(): pl.pallas_call(own_kernel(tiles_dev, groups, tile_rows, head_dim), out_sh...  2.68 us
  transfers between devices with their start and end apart: 2, of which 2 were waited for; matrix products, arithmetic and copies ran while one was open for 0% of the time, Pallas kernels for 23%

profile of v4, /device:TPU:0, one launch (start us, length us, event | category | flops | bytes accessed | tf_op | source)
XLA Modules:
  0.0 43.4 jit_solution(9288873577651660646)
XLA Ops:
  0.6 2.1 %pack.1 = (bf16[8,136,128]{2,1,0:T(8,128)(2,1)}, s32[8]{0:T(128)}) custom-call(s32[4,4,4]{2,1,0:T(4,128)} %picks_ref.7, bf16[512,256]{1,0:T(8,128)(2,1)} %q_hbm.3, bf16[512,256]{1,0:T(8,128)(2,1)} %g_hbm.3), custom_call_target="tpu_custom_call" | custom-call | tf_op jit(solution)/shard_map/pack/pallas_call | solution.py:739
  2.7 7.3 %all-to-all-start = ((bf16[8,136,128]{2,1,0:T(8,128)(2,1)}), bf16[8,136,128]{2,1,0:T(8,128)(2,1)S(1)}, u32[]{:S(2)}, u32[]{:S(2)}) async-start(bf16[8,136,128]{2,1,0:T(8,128)(2,1)} %get-tuple-element.19), calls=%async_computation | async-start | bytes 557056 | tf_op jit(solution)/shard_map/all_to_all | solution.py:746
  10.0 2.7 %own.1 = (bf16[4,512,128]{2,1,0:T(8,128)(2,1)S(1)}, bf16[4,128,512]{2,1,0:T(8,128)(2,1)S(1)}, f32[4,16,128]{2,1,0:T(8,128)S(1)}, f32[16,8,128]{2,1,0:T(8,128)S(1)}) custom-call(bf16[512,256]{1,0:T(8,128)(2,1)} %q_hbm.3, bf16[512,256]{1,0:T(8,128)(2,1)} %k_hbm.1, bf16[512,256]{1,0:T(8,128)(2,1)} %v_hbm.1, bf16[512,256]{1,0:T(8,128)(2,1)} %g_hbm.3), custom_call_target="tpu_custom_call" | custom-call | tf_op jit(solution)/shard_map/own/pallas_call | solution.py:748
  12.7 6.6 %all-to-all-done.recv_ref = bf16[8,136,128]{2,1,0:T(8,128)(2,1)S(1)} async-done(((bf16[8,136,128]{2,1,0:T(8,128)(2,1)}), bf16[8,136,128]{2,1,0:T(8,128)(2,1)S(1)}, u32[]{:S(2)}, u32[]{:S(2)}) %all-to-all-start) | async-done | bytes 278560 | tf_op jit(solution)/shard_map/all_to_all | solution.py:746
  19.3 3.3 %serve.1 = (bf16[8,216,128]{2,1,0:T(8,128)(2,1)}, f32[2,8,128]{2,1,0:T(8,128)S(1)}) custom-call(s32[4,4,4]{2,1,0:T(4,128)} %picks_ref.7, s32[8]{0:T(128)} %get-tuple-element.18.task_ref, bf16[8,136,128]{2,1,0:T(8,128)(2,1)S(1)} %all-to-all-done.recv_ref, bf16[4,512,128]{2,1,0:T(8,128)(2,1)S(1)} %get-tuple-element.20.kv_ref, ...), custom_call_target="tpu_custom_call" | custom-call | tf_op jit(solution)/shard_map/serve/pallas_call | solution.py:765
  22.6 3.6 %all-to-all-start.1 = ((bf16[8,216,128]{2,1,0:T(8,128)(2,1)}), bf16[8,216,128]{2,1,0:T(8,128)(2,1)S(1)}, u32[]{:S(2)}, u32[]{:S(2)}) async-start(bf16[8,216,128]{2,1,0:T(8,128)(2,1)} %get-tuple-element.25), calls=%async_computation.1 | async-start | bytes 884736 | tf_op jit(solution)/shard_map/all_to_all | solution.py:778
  26.2 5.7 %rest.1 = (bf16[4,128,512]{2,1,0:T(8,128)(2,1)}, bf16[4,4,192,128]{3,2,1,0:T(8,128)(2,1)}, bf16[4,512,1024]{2,1,0:T(8,128)(2,1)}) custom-call(bf16[512,256]{1,0:T(8,128)(2,1)} %q_hbm.3, bf16[512,256]{1,0:T(8,128)(2,1)} %g_hbm.3, bf16[4,512,128]{2,1,0:T(8,128)(2,1)S(1)} %get-tuple-element.20.kv_ref, bf16[4,128,512]{2,1,0:T(8,128)(2,1)S(1)} %get-tuple-element.21.vkt_ref, ...), custom_call_target="tpu_custom_call" | custom-call | tf_op jit(solution)/shard_map/rest/pallas_call | solution.py:792
  31.9 1.6 %again.1 = (bf16[7,512,256]{2,1,0:T(8,128)(2,1)S(1)}, bf16[7,128,128]{2,1,0:T(8,128)(2,1)S(1)}, f32[8,8,128]{2,1,0:T(8,128)S(1)}) custom-call(s32[4,4,4]{2,1,0:T(4,128)} %picks_ref.7, bf16[8,136,128]{2,1,0:T(8,128)(2,1)S(1)} %all-to-all-done.recv_ref, bf16[4,512,128]{2,1,0:T(8,128)(2,1)S(1)} %get-tuple-element.20.kv_ref, ...), custom_call_target="tpu_custom_call" | custom-call | tf_op jit(solution)/shard_map/again/pallas_call | solution.py:780
  33.4 5.2 %all-to-all-done.1.back_ref = bf16[8,216,128]{2,1,0:T(8,128)(2,1)S(1)} async-done(((bf16[8,216,128]{2,1,0:T(8,128)(2,1)}), bf16[8,216,128]{2,1,0:T(8,128)(2,1)S(1)}, u32[]{:S(2)}, u32[]{:S(2)}) %all-to-all-start.1) | async-done | bytes 442400 | tf_op jit(solution)/shard_map/all_to_all | solution.py:778
  38.6 4.8 %final.1 = (bf16[512,256]{1,0:T(8,128)(2,1)}, bf16[512,256]{1,0:T(8,128)(2,1)}, bf16[512,256]{1,0:T(8,128)(2,1)}, bf16[512,256]{1,0:T(8,128)(2,1)}) custom-call(s32[4,4,4]{2,1,0:T(4,128)} %picks_ref.7, s32[8]{0:T(128)} %get-tuple-element.18.task_ref, f32[8,8,128]{2,1,0:T(8,128)S(1)} %get-tuple-element.24.meta_ref, ...), custom_call_target="tpu_custom_call" | custom-call | tf_op jit(solution)/shard_map/final/pallas_call | solution.py:809
Async XLA Ops:
  2.7 16.6 %all-to-all-start = ((bf16[8,136,128]{2,1,0:T(8,128)(2,1)}), bf16[8,136,128]{2,1,0:T(8,128)(2,1)S(1)}, u32[]{:S(2)}, u32[]{:S(2)}) async-start(bf16[8,136,128]{2,1,0:T(8,128)(2,1)} %get-tuple-element.19), calls=%async_computation | async-start | bytes 557056 | tf_op jit(solution)/shard_map/all_to_all | solution.py:746
  22.6 16.0 %all-to-all-start.1 = ((bf16[8,216,128]{2,1,0:T(8,128)(2,1)}), bf16[8,216,128]{2,1,0:T(8,128)(2,1)S(1)}, u32[]{:S(2)}, u32[]{:S(2)}) async-start(bf16[8,216,128]{2,1,0:T(8,128)(2,1)} %get-tuple-element.25), calls=%async_computation.1 | async-start | bytes 884736 | tf_op jit(solution)/shard_map/all_to_all | solution.py:778
